TPU v7x, 256 devices: a whole 4x4x8 slice. The times are simulated.
256 devices in a mesh: freq: 128 (over x, y, z_hi, core), plane: 2 (over z_lo).
Axes of the slice: x: 4, y: 4, z: 8 (z_hi: 4, z_lo: 2; z = z_hi * 2 + z_lo), core: 2. Of those that a mesh axis runs over, the one named last changes fastest.
Arguments:
- state_in: float32 [2, 256, 5, 256, 128], P(None, 'freq', None, 'plane'), may hold values from -6 to 6
- forcing_in: float32 [2, 256, 5, 256, 128], P(None, 'freq', None, 'plane'), may hold values from -6 to 6
- base_flow: float32 [128, 5, 256, 128], P('freq', None, 'plane'), may hold values from -1 to 1
- station_index: int32 [2], replicated, may hold values from 0 to 127
- lobe_count: int32 [1], replicated, may hold values from 3 to 127
Outputs:
- state_out: float32 [2, 256, 5, 256, 128], P(None, 'freq', None, 'plane')
- forcing_out: float32 [2, 256, 5, 256, 128], P(None, 'freq', None, 'plane')
All inputs are finite; a program needn't handle non-finite values.
Results may differ from a plain program's by a relative error of at most 0.0003.
Values sent between devices are 32-bit elements; how exact they have to be, the bound alone decides.
No kernel may reach another device: no remote copies, remote signals or barrier semaphores. Data moves between devices by JAX's collectives and lax.ppermute only.
A program may use at most 128 MiB of HBM per device.

v0:
```python
import math

import jax
import jax.numpy as jnp
from jax import lax
from jax.sharding import PartitionSpec as P

SWEEPS = 4
STEPS = 2


SIDE_WEIGHT = 1.25
MARCH_WEIGHT = 4.0
DIAG_SHIFT = 4.0
ADVECT_SCALE = 0.5
BASE_SCALE = 0.5
HIGHEST_MODE = lax.Precision.HIGHEST


def broadcast(value, axis, source):
    kept = jnp.where(lax.axis_index(axis) == source, value, 0).astype(value.dtype)
    return lax.psum(kept, axis)


def padded_2(cells, sides, width):
    for axis, dim in sides:
        count = lax.axis_size(axis)
        head = lax.slice_in_dim(cells, 0, width, axis=dim)
        tail = lax.slice_in_dim(cells, cells.shape[dim] - width, cells.shape[dim], axis=dim)
        cells = jnp.concatenate(
            [
                lax.ppermute(tail, axis, [(i, (i + 1) % count) for i in range(count)]),
                cells,
                lax.ppermute(head, axis, [((i + 1) % count, i) for i in range(count)]),
            ],
            axis=dim,
        )
    return cells


def radial_tables(radius_count):
    indices = jnp.arange(radius_count)
    angles = math.pi * indices.astype(jnp.float32) / (radius_count - 1)
    cheb_nodes = jnp.cos(angles)
    weights = jnp.where((indices == 0) | (indices == radius_count - 1), 2.0, 1.0).astype(
        jnp.float32
    )
    parity = (1 - 2 * ((indices[:, None] + indices[None, :]) % 2)).astype(jnp.float32)
    offdiag = indices[:, None] != indices[None, :]
    spacing = jnp.where(offdiag, cheb_nodes[:, None] - cheb_nodes[None, :], 1.0)
    entries = jnp.where(offdiag, weights[:, None] / weights[None, :] * parity / spacing, 0.0)
    entries = entries - jnp.diag(jnp.sum(entries, axis=1))
    slopes = jnp.sin(angles)[:, None] * entries / (radius_count - 1)
    stiffness = jnp.dot(slopes.T, slopes, precision=HIGHEST_MODE)
    system = stiffness + DIAG_SHIFT * jnp.eye(radius_count, dtype=jnp.float32)
    factor = jnp.linalg.cholesky(system)
    factor_inv = lax.linalg.triangular_solve(
        factor, jnp.eye(radius_count, dtype=jnp.float32), left_side=True, lower=True
    )
    return (slopes, jnp.dot(factor_inv.T, factor_inv, precision=HIGHEST_MODE))


def transform_tables(freqs, ntime):
    mode_ids = jnp.arange(freqs)
    time_ids = jnp.arange(ntime)
    phases = mode_ids[:, None] * time_ids[None, :] % ntime
    angles = 2.0 * math.pi * phases.astype(jnp.float32) / ntime
    cosines = jnp.cos(angles)
    sine_tab = jnp.sin(angles)
    stacked = jnp.concatenate([cosines, -sine_tab], axis=0)
    return (stacked.T / math.sqrt(freqs), stacked / math.sqrt(ntime))


def chevron(lobe_count, azimuths, start_az, total_az):
    position = start_az + jnp.arange(azimuths)
    phases = lobe_count[0] * position % total_az
    return 1.0 + 0.5 * jnp.cos(2.0 * math.pi * phases.astype(jnp.float32) / total_az)


def relax_sweep(inner, neighbours, right_side, coefficient, omegas, inverse_p):
    real_part = inner[0]
    imag_part = inner[1]
    rate_col = omegas[:, None, None, None]
    scaled = coefficient[None]
    mixing = jnp.stack(
        [scaled * real_part - rate_col * imag_part, scaled * imag_part + rate_col * real_part]
    )
    summed = right_side - mixing + SIDE_WEIGHT * neighbours
    radius_count = summed.shape[-1]
    return jnp.dot(summed.reshape(-1, radius_count), inverse_p.T, precision=HIGHEST_MODE).reshape(
        summed.shape
    )


def advect(velocity, radial_time, around_time):
    carried = velocity[:, 1:2] * radial_time + velocity[:, 2:3] * around_time
    spread = velocity[:, 0] * (radial_time[:, 1] + around_time[:, 2])
    carried = jnp.concatenate([carried[:, 0:1] + spread[:, None], carried[:, 1:]], axis=1)
    return -ADVECT_SCALE * carried


def per_device(state_in, forcing_in, base_flow, station_index, lobe_count):
    per_dev = state_in.shape[1]
    variables = state_in.shape[2]
    span_az = state_in.shape[3]
    radius_count = state_in.shape[4]
    freqs = per_dev * lax.axis_size("freq")
    ntime = 3 * freqs // 2
    slopes, inverse_p = radial_tables(radius_count)
    inverse, forward = transform_tables(freqs, ntime)
    first_mode = lax.axis_index("freq") * per_dev
    omegas = 0.5 * (first_mode + jnp.arange(per_dev)).astype(jnp.float32) / freqs
    shape_az = chevron(
        lobe_count, span_az, lax.axis_index("plane") * span_az, span_az * lax.axis_size("plane")
    )
    stored = base_flow.shape[0]
    march_state = state_in
    forcing = forcing_in
    for station in range(STEPS):
        wanted = station_index[station]
        local_plane = lax.dynamic_index_in_dim(base_flow, wanted % stored, 0, keepdims=False)
        plane_flow = broadcast(local_plane, "freq", wanted // stored)
        coefficient = BASE_SCALE * plane_flow * shape_az[None, :, None]
        right_side = MARCH_WEIGHT * march_state + forcing
        iterate = march_state
        for sweep_no in range(SWEEPS):
            padded = padded_2(iterate, (("plane", 3),), 1)
            iterate = relax_sweep(
                iterate,
                padded[:, :, :, 2:] + padded[:, :, :, :-2],
                right_side,
                coefficient,
                omegas,
                inverse_p,
            )
        march_state = iterate
        rimmed = padded_2(march_state, (("plane", 3),), 1)
        beside_all = 0.5 * (rimmed[:, :, :, 2:] - rimmed[:, :, :, :-2])
        radial = jnp.dot(
            march_state.reshape(-1, radius_count), slopes.T, precision=HIGHEST_MODE
        ).reshape(march_state.shape)
        fields = jnp.stack([march_state, radial, beside_all])
        points = lax.all_to_all(fields, "freq", split_axis=4, concat_axis=2, tiled=True)
        in_time = jnp.einsum(
            "tc,kcx->ktx", inverse, points.reshape(3, 2 * freqs, -1), precision=HIGHEST_MODE
        ).reshape(3, ntime, variables, -1)
        velocity = in_time[0]
        radial_time = in_time[1]
        around_time = in_time[2]
        source = advect(velocity, radial_time, around_time)
        spectral = jnp.dot(forward, source.reshape(ntime, -1), precision=HIGHEST_MODE).reshape(
            2, freqs, variables, -1, radius_count
        )
        forcing = lax.all_to_all(spectral, "freq", split_axis=1, concat_axis=3, tiled=True)
    return (march_state, forcing)


def solution(mesh):
    return jax.shard_map(
        per_device,
        mesh=mesh,
        in_specs=(
            P(None, "freq", None, "plane", None),
            P(None, "freq", None, "plane", None),
            P("freq", None, "plane", None),
            P(),
            P(),
        ),
        out_specs=(P(None, "freq", None, "plane", None), P(None, "freq", None, "plane", None)),
        check_vma=False,
    )
```

profile of v0, /device:TPU:33, one launch (start us, length us, event | category | flops | bytes accessed | tf_op | source)
XLA Modules:
  0.0 1701.3 jit_solution(14322298090802658548)
XLA Ops:
  12.3 1.9 select_bitcast_fusion
  15.7 11.7 cholesky.18
  28.8 9.8 custom-call.6
  39.3 1247.6 %all-reduce.3.cloned.1.call-done = (f32[5,128,128]{2,1,0:T(8,128)}, f32[5,128,128]{2,1,0:T(8,128)}) async-done(((f32[5,128,128]{2,1,0:T(8,128)}, f32[5,128,128]{2,1,0:T(8,128)}), (f32[5,128,128]{2,1,0:T(8,128)}, f32[5,128,128]{2,1,0:T(8,128)})) %all-reduce.3.cloned.1.call-update) | async-done | bytes 655376 | tf_op jit(solution)/shard_map/psum | solution.py:22
  1311.4 4.9 copy.116
  1316.3 15.1 all-to-all-start
  1333.2 74.9 %all-to-all-done = f32[3,2,2,5,128,128]{5,2,3,1,0,4:T(2,128)} async-done(((f32[3,2,2,5,128,128]{5,2,3,1,0,4:T(2,128)}), f32[3,2,2,5,128,128]{5,2,3,1,0,4:T(2,128)}, u32[]{:S(2)}, u32[]{:S(2)}) %all-to-all-start) | async-done | bytes 3932192 | tf_op jit(solution)/shard_map/all_to_all | solution.py:143
  1408.1 5.6 copy.117
  1413.7 6.8 reshape.545
  1420.6 8.6 convolution_bitcast_fusion.1
  1429.7 2.5 convolution_bitcast_fusion.3
  1432.2 2.1 copy.119
  1434.3 22.2 %all-to-all-start.1 = ((f32[2,256,5,1,128]{4,0,3,2,1:T(2,128)}), f32[2,256,5,1,128]{4,0,3,2,1:T(2,128)S(1)}, u32[]{:S(2)}, u32[]{:S(2)}) async-start(f32[2,256,5,1,128]{4,0,3,2,1:T(2,128)} %copy.119), calls=%async_computation.1 | async-start | bytes 2621440 | tf_op jit(solution)/shard_map/all_to_all | solution.py:154
  1457.9 29.8 %all-to-all-done.1 = f32[2,256,5,1,128]{4,0,3,2,1:T(2,128)S(1)} async-done(((f32[2,256,5,1,128]{4,0,3,2,1:T(2,128)}), f32[2,256,5,1,128]{4,0,3,2,1:T(2,128)S(1)}, u32[]{:S(2)}, u32[]{:S(2)}) %all-to-all-start.1) | async-done | bytes 1310752 | tf_op jit(solution)/shard_map/all_to_all | solution.py:154
  1487.7 1.7 fusion.24
  1490.8 7.7 collective-permute-start.10
  1510.0 1.7 collective-permute-done.15
  1517.0 3.0 copy.122
  1520.0 104.5 %all_to_all.66 = f32[3,2,2,5,128,128]{5,2,3,1,0,4:T(2,128)S(1)} all-to-all(f32[3,2,2,5,128,128]{5,2,3,1,0,4:T(2,128)S(1)} %copy.122), channel_id=1, replica_groups=mesh['freq'=128,'plane'=2] {'freq'}, dimensions={4} | all-to-all | bytes 7864320 | tf_op jit(solution)/shard_map/all_to_all | solution.py:143
  1624.5 3.5 copy.123
  1628.0 6.9 reshape.555
  1634.9 8.6 convolution_bitcast_fusion
  1645.1 2.5 convolution_bitcast_fusion.2
  1648.6 44.4 %all_to_all.67 = f32[2,256,5,1,128]{4,0,3,2,1:T(2,128)S(1)} all-to-all(f32[2,256,5,1,128]{4,0,3,2,1:T(2,128)S(1)} %copy.125), channel_id=1, replica_groups=mesh['freq'=128,'plane'=2] {'freq'}, dimensions={1} | all-to-all | bytes 2621440 | tf_op jit(solution)/shard_map/all_to_all | solution.py:154
  (124 shorter events, 56.1 us)
Async XLA Ops:
  7.2 1279.8 %all-reduce.3.cloned.1.call-start = ((), (), s32[]{:S(2)}) async-start(), calls=%async_computation.4 | async-start | bytes 1310720 | tf_op jit(solution)/shard_map/psum | solution.py:22
  8.2 1280.3 %collective-permute-start = (f32[2,2,5,1,128]{4,3,2,1,0:T(1,128)S(1)}, f32[2,2,5,1,128]{4,3,2,1,0:T(1,128)S(1)}, u32[]{:S(2)}, u32[]{:S(2)}) collective-permute-start(f32[2,2,5,1,128]{4,3,2,1,0:T(1,128)S(1)} %get-tuple-element.56), channel_id=1, source_target_pairs={{1,0},{0,1},{3,2},{2,3},{5,4},{4,5},{7,6},{6,7},{9,8},{8,9},{11,10... | collective-permute-start | bytes 30728 | tf_op jit(solution)/shard_map/ppermute | solution.py:34
  8.3 1280.2 %collective-permute-start.1 = (f32[2,2,5,1,128]{4,3,2,1,0:T(1,128)S(1)}, f32[2,2,5,1,128]{4,3,2,1,0:T(1,128)S(1)}, u32[]{:S(2)}, u32[]{:S(2)}) collective-permute-start(f32[2,2,5,1,128]{4,3,2,1,0:T(1,128)S(1)} %get-tuple-element.57), channel_id=1, source_target_pairs={{0,1},{1,0},{2,3},{3,2},{4,5},{5,4},{6,7},{7,6},{8,9},{9,8},{10,11... | collective-permute-start | bytes 30728 | tf_op jit(solution)/shard_map/ppermute | solution.py:32
  15.6 1272.5 %copy-start = (f32[2,2,5,128,128]{4,3,2,1,0:T(8,128)S(1)}, f32[2,2,5,128,128]{4,3,2,1,0:T(8,128)}, u32[]{:S(2)}) copy-start(f32[2,2,5,128,128]{4,3,2,1,0:T(8,128)} %param.5) | copy-start | bytes 3932164
  1291.2 2.6 collective-permute-start.2
  1292.4 2.7 collective-permute-start.3
  1297.0 2.6 collective-permute-start.4
  1297.4 2.5 collective-permute-start.5
  1301.8 2.6 collective-permute-start.6
  1303.0 2.7 collective-permute-start.7
  1307.4 3.3 collective-permute-start.8
  1307.8 3.0 collective-permute-start.9
  1316.3 91.8 %all-to-all-start = ((f32[3,2,2,5,128,128]{5,2,3,1,0,4:T(2,128)}), f32[3,2,2,5,128,128]{5,2,3,1,0,4:T(2,128)}, u32[]{:S(2)}, u32[]{:S(2)}) async-start(f32[3,2,2,5,128,128]{5,2,3,1,0,4:T(2,128)} %copy.116), calls=%async_computation | async-start | bytes 7864320 | tf_op jit(solution)/shard_map/all_to_all | solution.py:143
  1333.1 87.5 %copy-start.5 = (f32[256,384]{1,0:T(8,128)}, f32[256,384]{1,0:T(8,128)S(1)}, u32[]{:S(2)}) copy-start(f32[256,384]{1,0:T(8,128)S(1)} %get-tuple-element.71) | copy-start | bytes 1179652
  1333.2 96.5 %copy-start.3 = (f32[512,384]{1,0:T(8,128)}, f32[512,384]{1,0:T(8,128)S(1)}, u32[]{:S(2)}) copy-start(f32[512,384]{1,0:T(8,128)S(1)} %fusion.37) | copy-start | bytes 2359300
  1434.3 53.4 %all-to-all-start.1 = ((f32[2,256,5,1,128]{4,0,3,2,1:T(2,128)}), f32[2,256,5,1,128]{4,0,3,2,1:T(2,128)S(1)}, u32[]{:S(2)}, u32[]{:S(2)}) async-start(f32[2,256,5,1,128]{4,0,3,2,1:T(2,128)} %copy.119), calls=%async_computation.1 | async-start | bytes 2621440 | tf_op jit(solution)/shard_map/all_to_all | solution.py:154
  1490.8 8.8 collective-permute-start.10
  1498.5 2.5 collective-permute-start.11
  1502.8 2.6 collective-permute-start.12
  1503.0 2.5 collective-permute-start.13
  1507.3 2.6 collective-permute-start.14
  1508.8 2.9 collective-permute-start.15
  1513.4 3.0 collective-permute-start.16
  1513.6 2.8 collective-permute-start.17
  (4 other events, 12.6 us)
Sparse Core Ops, SparseCore 0:
  14.3 1272.5 all-reduce.2
where the time goes:
time: 1710 us; the launch traced here: 1700 us
  waiting for transfers between devices  1360 us (80%)
  blocking collectives  149 us (9%)
  starting transfers between devices  58.6 us (3%)
  local copies, waits for them, and re-layouts  40.6 us (2%)
  other arithmetic  38.3 us (2%)
  matrix products  35.5 us (2%)
    psum x1, waiting for transfers between devices, broadcast(): return lax.psum(kept, axis)  1250 us
    all_to_all x1, blocking collectives, per_device(): lax.all_to_all(fields, 'freq', split_axis=4, concat_axis=2, tiled=True)  105 us
    all_to_all x1, waiting for transfers between devices, per_device(): lax.all_to_all(fields, 'freq', split_axis=4, concat_axis=2, tiled=True)  74.9 us
    all_to_all x1, blocking collectives, per_device(): lax.all_to_all(spectral, 'freq', split_axis=1, concat_axis=3, tiled=True)  44.4 us
  transfers between devices with their start and end apart: 21, of which 16 were waited for; matrix products, arithmetic and copies ran while one was open for 2% of the time, Pallas kernels for 0%

commit v1 on v0

v1 whole, which is shorter than its diff:
```python
import itertools
import math

import jax
import jax.numpy as jnp
import numpy as np
from jax import lax
from jax.experimental import pallas as pl
from jax.experimental.pallas import tpu as pltpu
from jax.sharding import PartitionSpec as P

SWEEPS = 4
STEPS = 2
SIDE_WEIGHT = 1.25
MARCH_WEIGHT = 4.0
DIAG_SHIFT = 4.0
ADVECT_SCALE = 0.5
BASE_SCALE = 0.5

NF = 128
PER = 2
NV = 5
AZ = 128
ALL_AZ = 256
R = 128
FREQS = NF * PER
NT = 3 * FREQS // 2
NC = 2 * PER * NV
HALO = 8
EXT = AZ + 2 * HALO
GUARD = 8
SLICE = 24


def freq_index(x, y, z, c):
    return ((x * 4 + y) * 4 + z) * 2 + c


def ring_orders():
    snake = [
        (x, y) for y in range(4) for x in (range(4) if y % 2 == 0 else range(3, -1, -1))
    ]
    cycle = [(0, 0), (1, 0), (2, 0), (3, 0), (3, 1), (3, 2), (3, 3), (2, 3)]
    cycle += [(2, 2), (2, 1), (1, 1), (1, 2), (1, 3), (0, 3), (0, 2), (0, 1)]

    def walk(start, end):
        i = cycle.index(start)
        forward = cycle[i:] + cycle[:i]
        if forward[-1] == end:
            return forward
        return [cycle[i]] + cycle[:i][::-1] + cycle[i + 1 :][::-1]

    first = []
    for z in range(4):
        first += [(x, y, z) for x, y in (snake if z % 2 == 0 else snake[::-1])]
    second = [(y, x, 3) for x, y in snake]
    second += [(x, y, 2) for x, y in walk((3, 0), (2, 0))]
    second += [(x, y, 1) for x, y in walk((2, 0), (1, 0))]
    second += [(x, y, 0) for x, y in walk((1, 0), (0, 0))]
    return [
        [freq_index(x, y, z, c) for x, y, z in path for c in (0, 1)]
        for path in (first, second)
    ]


ORDERS = ring_orders()
AZ_OF = np.argsort(np.array(ORDERS), axis=1).astype(np.int32)
RING = [f * 2 + p for p in (0, 1) for f in ORDERS[p]]
TO_NEXT = [(RING[i], RING[(i + 1) % ALL_AZ]) for i in range(ALL_AZ)]
TO_PREV = [(RING[(i + 1) % ALL_AZ], RING[i]) for i in range(ALL_AZ)]
SHEETS = [
    [freq_index(x, y, z, c) for x, y, c in itertools.product(range(4), range(4), range(2))]
    for z in range(4)
]


def z_shift(step):
    return [
        (freq_index(x, y, z, c), freq_index(x, y, (z + step) % 4, c))
        for x, y, z, c in itertools.product(range(4), range(4), range(4), range(2))
    ]


def split(table):
    table = np.asarray(table, np.float32)
    high = table.astype(jnp.bfloat16)
    low = (table - high.astype(np.float32)).astype(jnp.bfloat16)
    return high, low


def radial_tables():
    j = np.arange(R)
    phi = math.pi * j / (R - 1)
    x = np.cos(phi)
    c = np.where((j == 0) | (j == R - 1), 2.0, 1.0)
    parity = 1.0 - 2.0 * ((j[:, None] + j[None, :]) % 2)
    off = j[:, None] != j[None, :]
    gap = -2.0 * np.sin((phi[:, None] + phi[None, :]) / 2) * np.sin(
        (phi[:, None] - phi[None, :]) / 2
    )
    entries = np.where(off, c[:, None] / c[None, :] * parity / np.where(off, gap, 1.0), 0.0)
    entries = entries - np.diag(entries.sum(axis=1))
    slopes = np.sin(phi)[:, None] * entries / (R - 1)
    inverse = np.linalg.inv(slopes.T @ slopes + DIAG_SHIFT * np.eye(R))
    return slopes, inverse


def right_factor(matrix):
    high, low = split(np.asarray(matrix).T)
    half = np.concatenate([high, low], axis=1)
    return np.concatenate([half, half], axis=0)


def transform_tables():
    k = np.arange(FREQS)
    n = np.arange(NT)
    angle = 2.0 * math.pi * ((k[:, None] * n[None, :]) % NT) / NT
    table = np.stack([np.cos(angle), -np.sin(angle)])
    table = table.reshape(2, NF, PER, NT).transpose(1, 0, 2, 3).reshape(2 * FREQS, NT)
    inverse = np.concatenate(split(table.T / math.sqrt(FREQS)), axis=0)
    forward = np.concatenate(split(table / math.sqrt(NT)), axis=0)
    return inverse, forward


def halves(t):
    high = t.astype(jnp.bfloat16)
    low = (t - high.astype(jnp.float32)).astype(jnp.bfloat16)
    return jnp.concatenate([high, low], axis=1)


def along_radii(t, factor):
    both = jnp.dot(halves(t), factor, preferred_element_type=jnp.float32)
    return both[:, :R] + both[:, R:]


def transformed(table, t, rows):
    quad = jnp.dot(table, halves(t), preferred_element_type=jnp.float32)
    return (quad[:rows, :R] + quad[rows:, :R]) + (quad[:rows, R:] + quad[rows:, R:])


def march_kernel(last, *refs):
    if last:
        az_ref, om_ref, ext_ref, force_ref, fedge_ref, w_ref, q_ref = refs[:7]
        outs = refs[7:]
    else:
        az_ref, om_ref, state_ref, sedge_ref, force_ref, fedge_ref, w_ref, q_ref = refs[:8]
        outs = refs[8:]
    keep_ref, send_ref, it_ref, b_ref = outs
    for c in range(NC):
        at = GUARD + c * EXT
        own = pl.ds(c * AZ, AZ)
        head = pl.ds(c * 2 * HALO, HALO)
        tail = pl.ds(c * 2 * HALO + HALO, HALO)
        if last:
            it_ref[0, pl.ds(at, EXT), :] = ext_ref[pl.ds(c * EXT, EXT), :]
        else:
            it_ref[0, pl.ds(at, HALO), :] = sedge_ref[tail, :]
            it_ref[0, pl.ds(at + HALO, AZ), :] = state_ref[own, :]
            it_ref[0, pl.ds(at + HALO + AZ, HALO), :] = sedge_ref[head, :]
        for lo, size, part, ref in (
            (0, HALO, tail, fedge_ref),
            (HALO, AZ, own, force_ref),
            (HALO + AZ, HALO, head, fedge_ref),
        ):
            b_ref[pl.ds(c * EXT + lo, size), :] = (
                MARCH_WEIGHT * it_ref[0, pl.ds(at + lo, size), :] + ref[part, :]
            )

    factor = q_ref[...]

    def sweep(step, carry):
        now = lax.rem(step, 2)
        new = 1 - now
        for v in range(NV):
            w = w_ref[pl.ds(v * EXT, EXT), :]
            terms = [None] * 4
            for j in range(PER):
                rate = om_ref[j]
                planes = (j * NV + v, (PER + j) * NV + v)
                re, im = (it_ref[now, pl.ds(GUARD + c * EXT, EXT), :] for c in planes)
                for part, (c, mixed) in enumerate(
                    ((planes[0], w * re - rate * im), (planes[1], w * im + rate * re))
                ):
                    beside = (
                        it_ref[now, pl.ds(GUARD + c * EXT + 1, EXT), :]
                        + it_ref[now, pl.ds(GUARD + c * EXT - 1, EXT), :]
                    )
                    terms[part * PER + j] = (
                        b_ref[pl.ds(c * EXT, EXT), :] - mixed + SIDE_WEIGHT * beside
                    )
            done = along_radii(jnp.concatenate(terms, axis=0), factor)
            for i in range(4):
                it_ref[new, pl.ds(GUARD + (i * NV + v) * EXT, EXT), :] = done[
                    i * EXT : (i + 1) * EXT
                ]
        return carry

    lax.fori_loop(0, SWEEPS, sweep, 0)
    for c in range(NC):
        at = GUARD + c * EXT
        if last:
            keep_ref[pl.ds(c * AZ, AZ), :] = it_ref[0, pl.ds(at + HALO, AZ), :]
        else:
            keep_ref[pl.ds(c * EXT, EXT), :] = it_ref[0, pl.ds(at, EXT), :]
    final = it_ref.at[0]
    for f in range(NF):
        send_ref[pl.ds(f * NC, NC), :] = final[
            pl.ds(GUARD + HALO + az_ref[f], NC, stride=EXT), :
        ]


def to_time_kernel(points_ref, table_ref, u_ref):
    table = table_ref[...]

    def one(v, carry):
        x = points_ref[pl.ds(v, 2 * FREQS, stride=NV), :]
        u_ref[pl.ds(pl.multiple_of(v * NT, NT), NT), :] = transformed(table, x, NT)
        return carry

    lax.fori_loop(0, NV, one, 0)


def radial_kernel(u_ref, slope_ref, out_ref):
    factor = slope_ref[...]
    u0, u1 = u_ref[pl.ds(0, NT), :], u_ref[pl.ds(NT, NT), :]
    for v in (1, 0, 2, 3, 4):
        ur = along_radii(u_ref[pl.ds(v * NT, NT), :], factor)
        if v == 1:
            spread = u0 * ur
        carried = u1 * ur
        if v == 0:
            carried = carried + spread
        out_ref[pl.ds(v * NT, NT), :] = -ADVECT_SCALE * carried


def to_freq_kernel(u_ref, part_ref, next_ref, prev_ref, table_ref, out_ref):
    table = table_ref[...]
    u2 = u_ref[pl.ds(2 * NT, NT), :]

    def around(v):
        rows = pl.ds(pl.multiple_of(v * NT, NT), NT)
        return 0.5 * (next_ref[rows, :] - prev_ref[rows, :])

    def one(v, carry):
        rows = pl.ds(pl.multiple_of(v * NT, NT), NT)
        n = part_ref[rows, :] - ADVECT_SCALE * (u2 * around(v))
        extra = jnp.where(v == 0, ADVECT_SCALE, 0.0)
        n = n - extra * (u_ref[pl.ds(0, NT), :] * around(2))
        out_ref[pl.ds(v, 2 * FREQS, stride=NV), :] = transformed(table, n, 2 * FREQS)
        return carry

    lax.fori_loop(0, NV, one, 0)


def place_kernel(az_ref, got_ref, out_ref):
    for f in range(NF):
        out_ref[pl.ds(az_ref[f], NC, stride=AZ), :] = got_ref[pl.ds(f * NC, NC), :]


VMEM = pl.BlockSpec(memory_space=pltpu.VMEM)
SMEM = pl.BlockSpec(memory_space=pltpu.SMEM)


def call(kernel, specs, rows, name, flops, scratch=()):
    shapes = [jax.ShapeDtypeStruct((n, R), jnp.float32) for n in rows]
    return pl.pallas_call(
        kernel,
        in_specs=specs,
        out_specs=[VMEM] * len(rows) if len(rows) > 1 else VMEM,
        out_shape=shapes if len(rows) > 1 else shapes[0],
        scratch_shapes=list(scratch),
        compiler_params=pltpu.CompilerParams(vmem_limit_bytes=40 << 20),
        cost_estimate=pl.CostEstimate(
            flops=flops, bytes_accessed=4 * NC * AZ * R * 4, transcendentals=0
        ),
        name=name,
    )


def exchange(blocks):
    return lax.all_to_all(
        blocks.reshape(NF, NV, 4, R), "freq", split_axis=0, concat_axis=0, tiled=True
    ).reshape(NF * NC, R)


def edges(planes):
    count = planes.shape[0] // AZ
    planes = planes.reshape(count, AZ, R)
    mine = jnp.concatenate([planes[:, :HALO], planes[:, AZ - HALO :]], axis=1)
    return lax.ppermute(mine.reshape(-1, R), "plane", [(0, 1), (1, 0)])


def fetch_planes(base_flow, station_index):
    plane = base_flow.reshape(NV, AZ, R)
    beside = edges(plane.reshape(-1, R)).reshape(NV, 2 * HALO, R)
    whole = jnp.concatenate([beside[:, HALO:], plane, beside[:, :HALO]], axis=1)
    whole = whole.reshape(-1, R)
    whole = jnp.pad(whole, ((0, 32 * SLICE - whole.shape[0]), (0, 0)))
    held = lax.all_to_all(
        whole.reshape(32, SLICE, R),
        "freq",
        split_axis=0,
        concat_axis=0,
        tiled=True,
        axis_index_groups=SHEETS,
    )
    sheet = (station_index // 8) * 2 + station_index % 2
    mine = jnp.concatenate(
        [lax.dynamic_slice_in_dim(held, sheet[s], 1, axis=0) for s in range(STEPS)], axis=0
    )
    my_z = (lax.axis_index("freq") // 2) % 4
    behind = (my_z - station_index // 2) % 4
    chosen = mine
    for step in (1, 2, 3):
        came = lax.ppermute(mine, "freq", z_shift(step))
        chosen = jnp.where((behind == step)[:, None, None], came, chosen)
    spread = lax.all_to_all(
        jnp.broadcast_to(chosen[None], (32, STEPS, SLICE, R)),
        "freq",
        split_axis=0,
        concat_axis=0,
        tiled=True,
        axis_index_groups=SHEETS,
    )
    return [spread[:, s].reshape(-1, R)[: NV * EXT] for s in range(STEPS)]


def per_device(state_in, forcing_in, base_flow, station_index, lobe_count):
    slopes, inverse_p = radial_tables()
    solve = jnp.asarray(right_factor(inverse_p))
    slope = jnp.asarray(right_factor(slopes))
    inverse, forward = (jnp.asarray(t) for t in transform_tables())
    f = lax.axis_index("freq")
    p = lax.axis_index("plane")
    az_of = jnp.where(p == 0, jnp.asarray(AZ_OF[0]), jnp.asarray(AZ_OF[1]))
    omegas = 0.5 * (f * PER + jnp.arange(PER)).astype(jnp.float32) / FREQS
    position = (p * AZ - HALO + jnp.arange(EXT) + ALL_AZ) % ALL_AZ
    phases = lobe_count[0] * position % ALL_AZ
    shape_az = 1.0 + 0.5 * jnp.cos(2.0 * math.pi * phases.astype(jnp.float32) / ALL_AZ)
    shape_az = jnp.tile(shape_az, NV)[:, None]

    march = NC * AZ * R
    scratch = (
        pltpu.VMEM((2, NC * EXT + 2 * GUARD, R), jnp.float32),
        pltpu.VMEM((NC * EXT, R), jnp.float32),
    )
    state = state_in.reshape(NC * AZ, R)
    forcing = forcing_in.reshape(NC * AZ, R)
    state_edges = edges(state)
    planes = fetch_planes(base_flow, station_index)
    for station in range(STEPS):
        last = station == STEPS - 1
        weight = BASE_SCALE * planes[station] * shape_az
        forcing_edges = edges(forcing)
        start = (state,) if last else (state, state_edges)
        state, send = call(
            lambda *refs, last=last: march_kernel(last, *refs),
            [SMEM, SMEM] + [VMEM] * (len(start) + 4),
            (NC * (AZ if last else EXT), NC * AZ),
            "march",
            march * 2048,
            scratch,
        )(az_of, omegas, *start, forcing, forcing_edges, weight, solve)
        points = exchange(send)
        u = call(to_time_kernel, [VMEM] * 2, (NV * NT,), "to_time", march * 3072)(
            points, inverse
        )
        ahead = lax.ppermute(u, ("freq", "plane"), TO_PREV)
        behind = lax.ppermute(u, ("freq", "plane"), TO_NEXT)
        part = call(radial_kernel, [VMEM] * 2, (NV * NT,), "radial", march * 768)(u, slope)
        back = call(to_freq_kernel, [VMEM] * 5, (NC * AZ,), "to_freq", march * 3072)(
            u, part, ahead, behind, forward
        )
        got = exchange(back)
        forcing = call(place_kernel, [SMEM, VMEM], (NC * AZ,), "place", march)(az_of, got)
    return (state.reshape(state_in.shape), forcing.reshape(state_in.shape))


def solution(mesh):
    return jax.shard_map(
        per_device,
        mesh=mesh,
        in_specs=(
            P(None, "freq", None, "plane", None),
            P(None, "freq", None, "plane", None),
            P("freq", None, "plane", None),
            P(),
            P(),
        ),
        out_specs=(P(None, "freq", None, "plane", None), P(None, "freq", None, "plane", None)),
        check_vma=False,
    )
```

time: 1710 us -> 301 us (0.18)
  waiting for transfers between devices: 1360 us -> 51.2 us
  other arithmetic: 38.3 us -> 1.41 us
  matrix products: 35.5 us -> 0 us
  local copies, waits for them, and re-layouts: 40.6 us -> 5.36 us
  Pallas kernels: 0 us -> 29.3 us
  blocking collectives: 149 us -> 176 us
  starting transfers between devices: 58.6 us -> 31.6 us
    psum x1 -> x0, waiting for transfers between devices: 1250 us -> none  [broadcast(): return lax.psum(kept, axis)]
    all_to_all x2, waiting for transfers between devices: 105 us -> 18.1 us  [the longest x1 12.6 us: fetch_planes(): lax.all_to_all(jnp.broadcast_to(chosen[None], (32, STEPS, SLICE, R)), 'fr...]
    dot_general x16 -> x0, matrix products: 35.2 us -> none  [the longest x2 17.3 us: per_device(): jnp.einsum('tc,kcx->ktx', inverse, points.reshape(3, 2 * freqs, -1), prec...]
    pallas_call x0 -> x10, Pallas kernels: none -> 29.3 us  [the longest x2 15.2 us: per_device(): call(lambda *refs, last=last: march_kernel(last, *refs), [SMEM, SMEM] + [...]
    all_to_all x2 -> x4, blocking collectives: 149 us -> 176 us  [exchange(): lax.all_to_all(blocks.reshape(NF, NV, 4, R), 'freq', split_axis=0, concat...]
    another operation x9 -> x0, other arithmetic: 24.1 us -> none  [the longest x3 12.5 us: radial_tables(): factor = jnp.linalg.cholesky(system)]
    ppermute x18 -> x11, waiting for transfers between devices: 10 us -> 33.1 us  [the longest x2 21.2 us: per_device(): behind = lax.ppermute(u, ('freq', 'plane'), TO_NEXT)]
    all_to_all x2, starting transfers between devices: 37.3 us -> 15.1 us  [the longest x1 9.34 us: fetch_planes(): lax.all_to_all(whole.reshape(32, SLICE, R), 'freq', split_axis=0, concat_...]
  transfers between devices with their start and end apart: 21 -> 13, of which waited for: 16 -> 10; matrix products, arithmetic and copies ran while one was open for 2% -> 2% of each run, Pallas kernels for 0% -> 0%
where the time goes in v1:
time: 301 us; the launch traced here: 300 us
  blocking collectives  176 us (58%)
  waiting for transfers between devices  51.2 us (17%)
  starting transfers between devices  31.6 us (10%)
  Pallas kernels  29.3 us (10%)
  between operations  5.57 us (2%)
  local copies, waits for them, and re-layouts  5.36 us (2%)
    all_to_all x4, blocking collectives, exchange(): lax.all_to_all(blocks.reshape(NF, NV, 4, R), 'freq', split_axis=0, concat...  176 us
    ppermute x2, waiting for transfers between devices, per_device(): behind = lax.ppermute(u, ('freq', 'plane'), TO_NEXT)  21.2 us
    pallas_call x2, Pallas kernels, per_device(): call(lambda *refs, last=last: march_kernel(last, *refs), [SMEM, SMEM] + [...  15.2 us
    all_to_all x1, waiting for transfers between devices, fetch_planes(): lax.all_to_all(jnp.broadcast_to(chosen[None], (32, STEPS, SLICE, R)), 'fr...  12.6 us
    all_to_all x1, starting transfers between devices, fetch_planes(): lax.all_to_all(whole.reshape(32, SLICE, R), 'freq', split_axis=0, concat_...  9.34 us
    ppermute x3, starting transfers between devices, fetch_planes(): came = lax.ppermute(mine, 'freq', z_shift(step))  9.15 us
  transfers between devices with their start and end apart: 13, of which 10 were waited for; matrix products, arithmetic and copies ran while one was open for 2% of the time, Pallas kernels for 0%

profile of v1, /device:TPU:33, one launch (start us, length us, event | category | flops | bytes accessed | tf_op | source)
XLA Modules:
  0.0 300.0 jit_solution(2096513775164986767)
XLA Ops:
  6.1 9.3 %all-to-all-start = ((f32[32,24,128]{2,1,0:T(8,128)}), f32[32,24,128]{2,1,0:T(8,128)S(1)}, u32[]{:S(2)}, u32[]{:S(2)}) async-start(f32[32,24,128]{2,1,0:T(8,128)} %bitcast.10), calls=%async_computation | async-start | bytes 786432 | tf_op jit(solution)/shard_map/all_to_all | solution.py:299
  20.2 5.6 %all-to-all-done = f32[32,24,128]{2,1,0:T(8,128)S(1)} async-done(((f32[32,24,128]{2,1,0:T(8,128)}), f32[32,24,128]{2,1,0:T(8,128)S(1)}, u32[]{:S(2)}, u32[]{:S(2)}) %all-to-all-start) | async-done | bytes 393248 | tf_op jit(solution)/shard_map/all_to_all | solution.py:299
  25.8 3.0 collective-permute-start.5
  28.8 3.8 %collective-permute-start.4 = (f32[2,24,128]{2,1,0:T(8,128)S(1)}, f32[2,24,128]{2,1,0:T(8,128)S(1)}, u32[]{:S(2)}, u32[]{:S(2)}) collective-permute-start(f32[2,24,128]{2,1,0:T(8,128)S(1)} %pad_maximum_fusion.5), channel_id=1, source_target_pairs={{0,8},{2,10},{4,12},{6,14},{8,0},{10,2},{12,4},{14,6},{16,24},{18,... | collective-permute-start | bytes 73736 | tf_op jit(solution)/shard_map/ppermute | solution.py:315
  32.5 2.4 collective-permute-start.3
  37.3 5.8 %all-to-all-start.1 = ((f32[32,2,24,128]{3,2,1,0:T(8,128)}), f32[32,2,24,128]{3,2,1,0:T(8,128)}, u32[]{:S(2)}, u32[]{:S(2)}) async-start(f32[32,2,24,128]{3,2,1,0:T(8,128)} %broadcast_in_dim.30), calls=%async_computation.1 | async-start | bytes 1572864 | tf_op jit(solution)/shard_map/all_to_all | solution.py:317
  44.9 12.6 %all-to-all-done.1 = f32[32,2,24,128]{3,2,1,0:T(8,128)} async-done(((f32[32,2,24,128]{3,2,1,0:T(8,128)}), f32[32,2,24,128]{3,2,1,0:T(8,128)}, u32[]{:S(2)}, u32[]{:S(2)}) %all-to-all-start.1) | async-done | bytes 786464 | tf_op jit(solution)/shard_map/all_to_all | solution.py:317
  58.8 7.1 %march.2 = (f32[2880,128]{1,0:T(8,128)S(1)}, f32[2560,128]{1,0:T(8,128)S(1)}) custom-call(s32[128]{0:T(128)S(1)} %broadcast_select_fusion.refs_0_.az_ref, f32[2]{0:T(128)S(1)} %convert_multiply_fusion.refs_1_, f32[2560,128]{1,0:T(8,128)S(1)} %bitcast.37, f32[320,128]{1,0:T(8,128)S(1)} %collective-permute-done.refs_3_, f32[2560,128]{1,0:T(8,128)S(1)} %bitcast.39, ...), custom_call_target="tpu_custom_call" | custom-call | flops 671088640 | bytes 5242880 | tf_op jit(solution)/shard_map/march/pallas_call | solution.py:356
  66.0 45.2 %all_to_all.30 = f32[128,5,4,128]{3,2,1,0:T(4,128)S(1)} all-to-all(f32[128,5,4,128]{3,2,1,0:T(4,128)S(1)} %bitcast.41), channel_id=1, replica_groups=mesh['freq'=128,'plane'=2] {'freq'}, dimensions={0} | all-to-all | bytes 2621440 | tf_op jit(solution)/shard_map/all_to_all | solution.py:281
  113.1 2.6 collective-permute-start.7
  116.1 10.6 %collective-permute-done.7.prev_ref = f32[1920,128]{1,0:T(8,128)S(1)} collective-permute-done((f32[1920,128]{1,0:T(8,128)S(1)}, f32[1920,128]{1,0:T(8,128)S(1)}, u32[]{:S(2)}, u32[]{:S(2)}) %collective-permute-start.7) | collective-permute-done | bytes 983072 | tf_op jit(solution)/shard_map/ppermute | solution.py:369
  126.7 2.5 collective-permute-done.6.next_ref
  129.2 2.6 to_freq.2
  131.8 44.1 %all_to_all.31 = f32[128,5,4,128]{3,2,1,0:T(4,128)S(1)} all-to-all(f32[128,5,4,128]{3,2,1,0:T(4,128)S(1)} %bitcast.35), channel_id=1, replica_groups=mesh['freq'=128,'plane'=2] {'freq'}, dimensions={0} | all-to-all | bytes 2621440 | tf_op jit(solution)/shard_map/all_to_all | solution.py:281
  177.6 5.3 %collective-permute-done.8.refs_4_ = f32[320,128]{1,0:T(8,128)S(1)} collective-permute-done((f32[320,128]{1,0:T(8,128)S(1)}, f32[320,128]{1,0:T(8,128)S(1)}, u32[]{:S(2)}, u32[]{:S(2)}) %collective-permute-start.8) | collective-permute-done | bytes 163872 | tf_op jit(solution)/shard_map/ppermute | solution.py:290
  182.9 8.1 %march.3 = (f32[2560,128]{1,0:T(8,128)}, f32[2560,128]{1,0:T(8,128)S(1)}) custom-call(s32[128]{0:T(128)S(1)} %broadcast_select_fusion.refs_0_.az_ref, f32[2]{0:T(128)S(1)} %convert_multiply_fusion.refs_1_, f32[2880,128]{1,0:T(8,128)S(1)} %get-tuple-element.6.refs_2_, f32[2560,128]{1,0:T(8,128)S(1)} %place.2.refs_3_, ...), custom_call_target="tpu_custom_call" | custom-call | flops 671088640 | bytes 5242880 | tf_op jit(solution)/shard_map/march/pallas_call | solution.py:356
  191.0 43.9 %all_to_all.32 = f32[128,5,4,128]{3,2,1,0:T(4,128)S(1)} all-to-all(f32[128,5,4,128]{3,2,1,0:T(4,128)S(1)} %bitcast.40), channel_id=1, replica_groups=mesh['freq'=128,'plane'=2] {'freq'}, dimensions={0} | all-to-all | bytes 2621440 | tf_op jit(solution)/shard_map/all_to_all | solution.py:281
  234.9 1.9 to_time.3.u_ref
  236.8 2.1 collective-permute-start.10
  239.3 10.6 %collective-permute-done.10.prev_ref = f32[1920,128]{1,0:T(8,128)S(1)} collective-permute-done((f32[1920,128]{1,0:T(8,128)S(1)}, f32[1920,128]{1,0:T(8,128)S(1)}, u32[]{:S(2)}, u32[]{:S(2)}) %collective-permute-start.10) | collective-permute-done | bytes 983072 | tf_op jit(solution)/shard_map/ppermute | solution.py:369
  249.9 2.5 collective-permute-done.9.next_ref
  252.4 2.5 to_freq.3
  254.9 42.4 %all_to_all.33 = f32[128,5,4,128]{3,2,1,0:T(4,128)S(1)} all-to-all(f32[128,5,4,128]{3,2,1,0:T(4,128)S(1)} %bitcast.34), channel_id=1, replica_groups=mesh['freq'=128,'plane'=2] {'freq'}, dimensions={0} | all-to-all | bytes 2621440 | tf_op jit(solution)/shard_map/all_to_all | solution.py:281
  297.4 2.7 place.3
  (60 shorter events, 15.5 us)
Async XLA Ops:
  1.4 2.9 collective-permute-start.2
  2.4 13.0 %copy-start.6 = (s32[2]{0:T(128)S(1)}, s32[2]{0:T(128)}, u32[]{:S(2)}) copy-start(s32[2]{0:T(128)} %param.14) | copy-start | bytes 28
  2.5 56.3 %collective-permute-start = (f32[320,128]{1,0:T(8,128)S(1)}, f32[320,128]{1,0:T(8,128)S(1)}, u32[]{:S(2)}, u32[]{:S(2)}) collective-permute-start(f32[320,128]{1,0:T(8,128)S(1)} %bitcast.48), channel_id=1, source_target_pairs={{0,1},{1,0},{2,3},{3,2},{4,5},{5,4},{6,7},{7,6},{8,9},{9,8},{10,11... | collective-permute-start | bytes 491528 | tf_op jit(solution)/shard_map/ppermute | solution.py:290
  6.1 19.7 %all-to-all-start = ((f32[32,24,128]{2,1,0:T(8,128)}), f32[32,24,128]{2,1,0:T(8,128)S(1)}, u32[]{:S(2)}, u32[]{:S(2)}) async-start(f32[32,24,128]{2,1,0:T(8,128)} %bitcast.10), calls=%async_computation | async-start | bytes 786432 | tf_op jit(solution)/shard_map/all_to_all | solution.py:299
  20.1 22.9 %copy-start.2 = (f32[2,2,5,128,128]{4,3,2,1,0:T(8,128)S(1)}, f32[2,2,5,128,128]{4,3,2,1,0:T(8,128)}, u32[]{:S(2)}) copy-start(f32[2,2,5,128,128]{4,3,2,1,0:T(8,128)} %param.12) | copy-start | bytes 3932164
  25.8 9.2 %collective-permute-start.5 = (f32[2,24,128]{2,1,0:T(8,128)S(1)}, f32[2,24,128]{2,1,0:T(8,128)S(1)}, u32[]{:S(2)}, u32[]{:S(2)}) collective-permute-start(f32[2,24,128]{2,1,0:T(8,128)S(1)} %pad_maximum_fusion.5), channel_id=1, source_target_pairs={{0,4},{2,6},{4,8},{6,10},{8,12},{10,14},{12,0},{14,2},{16,20},{18,... | collective-permute-start | bytes 73736 | tf_op jit(solution)/shard_map/ppermute | solution.py:315
  28.8 6.6 %collective-permute-start.4 = (f32[2,24,128]{2,1,0:T(8,128)S(1)}, f32[2,24,128]{2,1,0:T(8,128)S(1)}, u32[]{:S(2)}, u32[]{:S(2)}) collective-permute-start(f32[2,24,128]{2,1,0:T(8,128)S(1)} %pad_maximum_fusion.5), channel_id=1, source_target_pairs={{0,8},{2,10},{4,12},{6,14},{8,0},{10,2},{12,4},{14,6},{16,24},{18,... | collective-permute-start | bytes 73736 | tf_op jit(solution)/shard_map/ppermute | solution.py:315
  32.5 3.7 %collective-permute-start.3 = (f32[2,24,128]{2,1,0:T(8,128)S(1)}, f32[2,24,128]{2,1,0:T(8,128)S(1)}, u32[]{:S(2)}, u32[]{:S(2)}) collective-permute-start(f32[2,24,128]{2,1,0:T(8,128)S(1)} %pad_maximum_fusion.5), channel_id=1, source_target_pairs={{0,12},{2,14},{4,0},{6,2},{8,4},{10,6},{12,8},{14,10},{16,28},{18,... | collective-permute-start | bytes 73736 | tf_op jit(solution)/shard_map/ppermute | solution.py:315
  37.3 7.6 %copy-start.7 = (s32[128]{0:T(128)S(1)}, s32[128]{0:T(128)}, u32[]{:S(2)}) copy-start(s32[128]{0:T(128)} %constant.134.clone) | copy-start | bytes 1540
  37.3 7.6 %copy-start.8 = (s32[128]{0:T(128)S(1)}, s32[128]{0:T(128)}, u32[]{:S(2)}) copy-start(s32[128]{0:T(128)} %constant.133.clone) | copy-start | bytes 1540
  37.3 20.2 %all-to-all-start.1 = ((f32[32,2,24,128]{3,2,1,0:T(8,128)}), f32[32,2,24,128]{3,2,1,0:T(8,128)}, u32[]{:S(2)}, u32[]{:S(2)}) async-start(f32[32,2,24,128]{3,2,1,0:T(8,128)} %broadcast_in_dim.30), calls=%async_computation.1 | async-start | bytes 1572864 | tf_op jit(solution)/shard_map/all_to_all | solution.py:317
  43.1 15.7 %collective-permute-start.1 = (f32[320,128]{1,0:T(8,128)S(1)}, f32[320,128]{1,0:T(8,128)S(1)}, u32[]{:S(2)}, u32[]{:S(2)}) collective-permute-start(f32[320,128]{1,0:T(8,128)S(1)} %bitcast.49), channel_id=1, source_target_pairs={{0,1},{1,0},{2,3},{3,2},{4,5},{5,4},{6,7},{7,6},{8,9},{9,8},{10,11... | collective-permute-start | bytes 491528 | tf_op jit(solution)/shard_map/ppermute | solution.py:290
  44.9 13.9 %copy-start.1 = (f32[2,2,5,128,128]{4,3,2,1,0:T(8,128)S(1)}, f32[2,2,5,128,128]{4,3,2,1,0:T(8,128)}, u32[]{:S(2)}) copy-start(f32[2,2,5,128,128]{4,3,2,1,0:T(8,128)} %param.11) | copy-start | bytes 3932164
  44.9 13.9 %copy-start.4 = (bf16[256,256]{1,0:T(8,128)(2,1)S(1)}, bf16[256,256]{1,0:T(8,128)(2,1)}, u32[]{:S(2)}) copy-start(bf16[256,256]{1,0:T(8,128)(2,1)} %constant.129.clone.refs_7_.refs_6_) | copy-start | bytes 393220
  66.0 45.2 %copy-start.5 = (bf16[768,512]{1,0:T(8,128)(2,1)S(1)}, bf16[768,512]{1,0:T(8,128)(2,1)}, u32[]{:S(2)}) copy-start(bf16[768,512]{1,0:T(8,128)(2,1)} %constant.131.clone.table_ref) | copy-start | bytes 2359300
  111.1 4.5 %copy-start.3 = (bf16[256,256]{1,0:T(8,128)(2,1)S(1)}, bf16[256,256]{1,0:T(8,128)(2,1)}, u32[]{:S(2)}) copy-start(bf16[256,256]{1,0:T(8,128)(2,1)} %constant.130.clone.slope_ref) | copy-start | bytes 393220
  113.1 16.1 %copy-start = (bf16[1024,384]{1,0:T(8,128)(2,1)S(1)}, bf16[1024,384]{1,0:T(8,128)(2,1)}, u32[]{:S(2)}) copy-start(bf16[1024,384]{1,0:T(8,128)(2,1)} %constant.132.clone.table_ref) | copy-start | bytes 2359300
  113.1 13.6 %collective-permute-start.7 = (f32[1920,128]{1,0:T(8,128)S(1)}, f32[1920,128]{1,0:T(8,128)S(1)}, u32[]{:S(2)}, u32[]{:S(2)}) collective-permute-start(f32[1920,128]{1,0:T(8,128)S(1)} %to_time.2.u_ref), channel_id=1, source_target_pairs={{0,2},{2,64},{64,66},{66,128},{128,130},{130,192},{192,194},{194,2... | collective-permute-start | bytes 2949128 | tf_op jit(solution)/shard_map/ppermute | solution.py:369
  115.7 13.5 %collective-permute-start.6 = (f32[1920,128]{1,0:T(8,128)S(1)}, f32[1920,128]{1,0:T(8,128)S(1)}, u32[]{:S(2)}, u32[]{:S(2)}) collective-permute-start(f32[1920,128]{1,0:T(8,128)S(1)} %to_time.2.u_ref), channel_id=1, source_target_pairs={{2,0},{64,2},{66,64},{128,66},{130,128},{192,130},{194,192},{208,1... | collective-permute-start | bytes 2949128 | tf_op jit(solution)/shard_map/ppermute | solution.py:368
  177.5 5.4 %collective-permute-start.8 = (f32[320,128]{1,0:T(8,128)S(1)}, f32[320,128]{1,0:T(8,128)S(1)}, u32[]{:S(2)}, u32[]{:S(2)}) collective-permute-start(f32[320,128]{1,0:T(8,128)S(1)} %bitcast.50), channel_id=1, source_target_pairs={{0,1},{1,0},{2,3},{3,2},{4,5},{5,4},{6,7},{7,6},{8,9},{9,8},{10,11... | collective-permute-start | bytes 491528 | tf_op jit(solution)/shard_map/ppermute | solution.py:290
  236.8 13.1 %collective-permute-start.10 = (f32[1920,128]{1,0:T(8,128)S(1)}, f32[1920,128]{1,0:T(8,128)S(1)}, u32[]{:S(2)}, u32[]{:S(2)}) collective-permute-start(f32[1920,128]{1,0:T(8,128)S(1)} %to_time.3.u_ref), channel_id=1, source_target_pairs={{0,2},{2,64},{64,66},{66,128},{128,130},{130,192},{192,194},{194,2... | collective-permute-start | bytes 2949128 | tf_op jit(solution)/shard_map/ppermute | solution.py:369
  238.9 13.5 %collective-permute-start.9 = (f32[1920,128]{1,0:T(8,128)S(1)}, f32[1920,128]{1,0:T(8,128)S(1)}, u32[]{:S(2)}, u32[]{:S(2)}) collective-permute-start(f32[1920,128]{1,0:T(8,128)S(1)} %to_time.3.u_ref), channel_id=1, source_target_pairs={{2,0},{64,2},{66,64},{128,66},{130,128},{192,130},{194,192},{208,1... | collective-permute-start | bytes 2949128 | tf_op jit(solution)/shard_map/ppermute | solution.py:368

commit v2 on v1

v2 whole, which is shorter than its diff:
```python
import itertools
import math

import jax
import jax.numpy as jnp
import numpy as np
from jax import lax
from jax.experimental import pallas as pl
from jax.experimental.pallas import tpu as pltpu
from jax.sharding import PartitionSpec as P

SWEEPS = 4
STEPS = 2
SIDE_WEIGHT = 1.25
MARCH_WEIGHT = 4.0
DIAG_SHIFT = 4.0
ADVECT_SCALE = 0.5
BASE_SCALE = 0.5

NF = 128
PER = 2
NV = 5
AZ = 128
ALL_AZ = 256
R = 128
FREQS = NF * PER
NT = 3 * FREQS // 2
NC = 2 * PER * NV
HALO = 8
EXT = AZ + 2 * HALO
GUARD = 8
KEPT = 2 * FREQS
CHUNKS = ((0, 1, 2), (3, 4))
COST = 1e8


def freq_index(x, y, z, c):
    return ((x * 4 + y) * 4 + z) * 2 + c


def ring_orders():
    snake = [
        (x, y) for y in range(4) for x in (range(4) if y % 2 == 0 else range(3, -1, -1))
    ]
    cycle = [(0, 0), (1, 0), (2, 0), (3, 0), (3, 1), (3, 2), (3, 3), (2, 3)]
    cycle += [(2, 2), (2, 1), (1, 1), (1, 2), (1, 3), (0, 3), (0, 2), (0, 1)]

    def walk(start, end):
        i = cycle.index(start)
        forward = cycle[i:] + cycle[:i]
        if forward[-1] == end:
            return forward
        return [cycle[i]] + cycle[:i][::-1] + cycle[i + 1 :][::-1]

    first = []
    for z in range(4):
        first += [(x, y, z) for x, y in (snake if z % 2 == 0 else snake[::-1])]
    second = [(y, x, 3) for x, y in snake]
    second += [(x, y, 2) for x, y in walk((3, 0), (2, 0))]
    second += [(x, y, 1) for x, y in walk((2, 0), (1, 0))]
    second += [(x, y, 0) for x, y in walk((1, 0), (0, 0))]
    return [
        [freq_index(x, y, z, c) for x, y, z in path for c in (0, 1)]
        for path in (first, second)
    ]


ORDERS = ring_orders()
AZ_OF = np.argsort(np.array(ORDERS), axis=1).astype(np.int32)
RING = [f * 2 + p for p in (0, 1) for f in ORDERS[p]]
TO_NEXT = [(RING[i], RING[(i + 1) % ALL_AZ]) for i in range(ALL_AZ)]
TO_PREV = [(RING[(i + 1) % ALL_AZ], RING[i]) for i in range(ALL_AZ)]
FLAT = [[g * 8 + s for g in range(16)] for s in range(8)]
TALL = [[g * 8 + s for s in range(8)] for g in range(16)]
EDGE_AT = np.array(
    [[ORDERS[p][a] for a in (*range(HALO), *range(AZ - HALO, AZ))] for p in (0, 1)], np.int32
)


def split(table):
    table = np.asarray(table, np.float32)
    high = table.astype(jnp.bfloat16)
    low = (table - high.astype(np.float32)).astype(jnp.bfloat16)
    return high, low


def radial_tables():
    j = np.arange(R)
    phi = math.pi * j / (R - 1)
    x = np.cos(phi)
    c = np.where((j == 0) | (j == R - 1), 2.0, 1.0)
    parity = 1.0 - 2.0 * ((j[:, None] + j[None, :]) % 2)
    off = j[:, None] != j[None, :]
    gap = -2.0 * np.sin((phi[:, None] + phi[None, :]) / 2) * np.sin(
        (phi[:, None] - phi[None, :]) / 2
    )
    entries = np.where(off, c[:, None] / c[None, :] * parity / np.where(off, gap, 1.0), 0.0)
    entries = entries - np.diag(entries.sum(axis=1))
    slopes = np.sin(phi)[:, None] * entries / (R - 1)
    inverse = np.linalg.inv(slopes.T @ slopes + DIAG_SHIFT * np.eye(R))
    return slopes, inverse


def right_factor(matrix):
    high, low = split(np.asarray(matrix).T)
    half = np.concatenate([high, low], axis=1)
    return np.concatenate([half, half], axis=0)


def transform_tables():
    k = np.arange(FREQS)
    n = np.arange(NT)
    angle = 2.0 * math.pi * ((k[:, None] * n[None, :]) % NT) / NT
    table = np.stack([np.cos(angle), -np.sin(angle)])
    table = table.reshape(2, NF, PER, NT).transpose(0, 2, 1, 3).reshape(2 * FREQS, NT)
    inverse = np.concatenate(split(table.T / math.sqrt(FREQS)), axis=0)
    forward = np.concatenate(split(table / math.sqrt(NT)), axis=0)
    return inverse, forward


def halves(t):
    high = t.astype(jnp.bfloat16)
    low = (t - high.astype(jnp.float32)).astype(jnp.bfloat16)
    return jnp.concatenate([high, low], axis=1)


def along_radii(t, factor):
    both = jnp.dot(halves(t), factor, preferred_element_type=jnp.float32)
    return both[:, :R] + both[:, R:]


def transformed(table, t, rows):
    quad = jnp.dot(table, halves(t), preferred_element_type=jnp.float32)
    return (quad[:rows, :R] + quad[rows:, :R]) + (quad[:rows, R:] + quad[rows:, R:])


def march_kernel(
    az_ref, om_ref, state_ref, sedge_ref, force_ref, fedge_ref,
    plane_ref, pedge_ref, shape_ref, q_ref, send_ref, it_ref, b_ref, w_ref
):
    for n in range(AZ):
        w_ref[pl.ds(HALO + az_ref[n], NV, stride=EXT), :] = plane_ref[pl.ds(n * NV, NV), :]
    for v in range(NV):
        at = v * 2 * HALO
        w_ref[pl.ds(v * EXT, HALO), :] = pedge_ref[pl.ds(at + HALO, HALO), :]
        w_ref[pl.ds(v * EXT + HALO + AZ, HALO), :] = pedge_ref[pl.ds(at, HALO), :]
    for v in range(NV):
        rows = pl.ds(v * EXT, EXT)
        w_ref[rows, :] = w_ref[rows, :] * shape_ref[...]
    for c in range(NC):
        at = GUARD + c * EXT
        own = pl.ds(c * AZ, AZ)
        head = pl.ds(c * 2 * HALO, HALO)
        tail = pl.ds(c * 2 * HALO + HALO, HALO)
        for lo, size, part, ref, add_ref in (
            (0, HALO, tail, sedge_ref, fedge_ref),
            (HALO, AZ, own, state_ref, force_ref),
            (HALO + AZ, HALO, head, sedge_ref, fedge_ref),
        ):
            q = ref[part, :]
            it_ref[0, pl.ds(at + lo, size), :] = q
            b_ref[pl.ds(c * EXT + lo, size), :] = MARCH_WEIGHT * q + add_ref[part, :]

    factor = q_ref[...]

    def sweep(step, carry):
        now = lax.rem(step, 2)
        new = 1 - now
        for v in range(NV):
            w = w_ref[pl.ds(v * EXT, EXT), :]
            terms = [None] * 4
            for j in range(PER):
                rate = om_ref[j]
                planes = (j * NV + v, (PER + j) * NV + v)
                re, im = (it_ref[now, pl.ds(GUARD + c * EXT, EXT), :] for c in planes)
                for part, (c, mixed) in enumerate(
                    ((planes[0], w * re - rate * im), (planes[1], w * im + rate * re))
                ):
                    beside = (
                        it_ref[now, pl.ds(GUARD + c * EXT + 1, EXT), :]
                        + it_ref[now, pl.ds(GUARD + c * EXT - 1, EXT), :]
                    )
                    terms[part * PER + j] = (
                        b_ref[pl.ds(c * EXT, EXT), :] - mixed + SIDE_WEIGHT * beside
                    )
            done = along_radii(jnp.concatenate(terms, axis=0), factor)
            for i in range(4):
                it_ref[new, pl.ds(GUARD + (i * NV + v) * EXT, EXT), :] = done[
                    i * EXT : (i + 1) * EXT
                ]
        return carry

    lax.fori_loop(0, SWEEPS, sweep, 0)
    final = it_ref.at[0]
    for f in range(NF):
        send_ref[pl.ds(f * NC, NC), :] = final[
            pl.ds(GUARD + HALO + az_ref[f], NC, stride=EXT), :
        ]


def rows_of(v, size):
    return pl.ds(pl.multiple_of(v * size, size), size)


def unpack_kernel(points_ref, table_ref, *out_refs):
    table = table_ref[...]
    count = len(CHUNKS)
    for vs, x_ref, u_ref in zip(CHUNKS, out_refs[:count], out_refs[count:]):

        def one(at, carry, first=vs[0], x_ref=x_ref, u_ref=u_ref):
            x = jnp.concatenate(
                [
                    points_ref[pl.ds(i * NV + first + at, NF, stride=NC), :]
                    for i in range(2 * PER)
                ],
                axis=0,
            )
            x_ref[rows_of(at, KEPT), :] = x
            u_ref[rows_of(at, NT), :] = transformed(table, x, NT)
            return carry

        lax.fori_loop(0, len(vs), one, 0)


def radial_kernel(first, *refs):
    lead_ref, u_ref = (refs[0], refs[0]) if first else refs[:2]
    slope_ref, out_ref = refs[-2:]
    factor = slope_ref[...]
    u1 = lead_ref[pl.ds(NT, NT), :]
    for at in range(u_ref.shape[0] // NT):
        ur = along_radii(u_ref[pl.ds(at * NT, NT), :], factor)
        out_ref[pl.ds(at * NT, NT), :] = -ADVECT_SCALE * (u1 * ur)
        if first and at == 1:
            out_ref[pl.ds(0, NT), :] = out_ref[pl.ds(0, NT), :] - ADVECT_SCALE * (
                lead_ref[pl.ds(0, NT), :] * ur
            )


def sweep_rows(q, b, beside, w, rate, factor):
    re, im = q[:FREQS], q[FREQS:]
    mixed = jnp.concatenate([w * re - rate * im, w * im + rate * re], axis=0)
    return along_radii(b - mixed + SIDE_WEIGHT * beside, factor)


def rates():
    row = lax.broadcasted_iota(jnp.int32, (FREQS, R), 0)
    return (PER * (row & (NF - 1)) + (row >> 7)).astype(jnp.float32) * (0.5 / FREQS)


def forcing_kernel(
    first, lead_ref, part_ref, x_ref, next_ref, prev_ref, w_ref, inv_ref, fwd_ref, q_ref,
    new_ref, b_ref, *around_ref
):
    inverse, forward, factor = inv_ref[...], fwd_ref[...], q_ref[...]
    rate = rates()

    def around(v):
        rows = rows_of(v, KEPT)
        return transformed(inverse, 0.5 * (next_ref[rows, :] - prev_ref[rows, :]), NT)

    if first:
        around_ref[0][...] = around(2)

    def one(at, carry):
        rows, times = rows_of(at, KEPT), rows_of(at, NT)
        n = part_ref[times, :] - ADVECT_SCALE * (lead_ref[pl.ds(2 * NT, NT), :] * around(at))
        if first:
            extra = jnp.where(at == 0, ADVECT_SCALE, 0.0)
            n = n - extra * (lead_ref[pl.ds(0, NT), :] * around_ref[0][...])
        x = x_ref[rows, :]
        b = MARCH_WEIGHT * x + transformed(forward, n, KEPT)
        b_ref[rows, :] = b
        beside = next_ref[rows, :] + prev_ref[rows, :]
        new_ref[rows, :] = sweep_rows(x, b, beside, w_ref[pl.ds(at, 1), :], rate, factor)
        return carry

    lax.fori_loop(0, x_ref.shape[0] // KEPT, one, 0)


def sweep_kernel(x_ref, next_ref, prev_ref, b_ref, w_ref, q_ref, *more):
    factor = q_ref[...]
    rate = rates()
    new_ref = more[-2] if len(more) > 1 else more[-1]

    def one(at, carry):
        rows = rows_of(at, KEPT)
        beside = next_ref[rows, :] + prev_ref[rows, :]
        x = sweep_rows(
            x_ref[rows, :], b_ref[rows, :], beside, w_ref[pl.ds(at, 1), :], rate, factor
        )
        new_ref[rows, :] = x
        if len(more) > 1:
            more[-1][rows_of(at, NT), :] = transformed(more[0][...], x, NT)
        return carry

    lax.fori_loop(0, x_ref.shape[0] // KEPT, one, 0)


def pack_kernel(*refs):
    send_ref = refs[-1]
    for vs, x_ref in zip(CHUNKS, refs):
        for at, v in enumerate(vs):
            for i in range(2 * PER):
                send_ref[pl.ds(i * NV + v, NF, stride=2 * NC), :] = x_ref[
                    pl.ds(at * KEPT + i * NF, NF), :
                ]


def to_freq_kernel(*refs):
    count = len(CHUNKS)
    u_ref, fwd_ref, out_ref = refs[0], refs[-3], refs[-1]
    forward = fwd_ref[...]
    u2 = u_ref[pl.ds(2 * NT, NT), :]
    lead_next, lead_prev = refs[1 + count], refs[1 + 2 * count]
    for n, vs in enumerate(CHUNKS):
        part_ref, next_ref, prev_ref = (refs[1 + n + m * count] for m in range(3))

        def one(at, carry, first=vs[0], part=part_ref, ahead=next_ref, behind=prev_ref):
            rows = rows_of(at, NT)
            n = part[rows, :] - ADVECT_SCALE * (u2 * (0.5 * (ahead[rows, :] - behind[rows, :])))
            if first == 0:
                two = pl.ds(2 * NT, NT)
                around = 0.5 * (lead_next[two, :] - lead_prev[two, :])
                extra = jnp.where(at == 0, ADVECT_SCALE, 0.0)
                n = n - extra * (u_ref[pl.ds(0, NT), :] * around)
            g = transformed(forward, n, KEPT)
            for i in range(2 * PER):
                out_ref[pl.ds(NC + i * NV + first + at, NF, stride=2 * NC), :] = g[
                    i * NF : (i + 1) * NF
                ]
            return carry

        lax.fori_loop(0, len(vs), one, 0)


def place_kernel(az_ref, got_ref, state_ref, forcing_ref):
    for f in range(NF):
        to = pl.ds(az_ref[f], NC, stride=AZ)
        state_ref[to, :] = got_ref[pl.ds(f * 2 * NC, NC), :]
        forcing_ref[to, :] = got_ref[pl.ds(f * 2 * NC + NC, NC), :]


def sort_kernel(az_ref, plane_ref, out_ref):
    for n in range(AZ):
        out_ref[pl.ds(n * NV, NV), :] = plane_ref[pl.ds(az_ref[n], NV, stride=AZ), :]


def rim_kernel(at_ref, plane_ref, out_ref):
    for e in range(2 * HALO):
        out_ref[pl.ds(e, NV, stride=2 * HALO), :] = plane_ref[pl.ds(at_ref[e] * NV, NV), :]


ANY = pl.BlockSpec(memory_space=pl.ANY)
VMEM = pl.BlockSpec(memory_space=pltpu.VMEM)
SMEM = pl.BlockSpec(memory_space=pltpu.SMEM)


def call(kernel, specs, rows, name, work, scratch=(), aliases=None):
    shapes = [jax.ShapeDtypeStruct((n, R), jnp.float32) for n in rows]
    return pl.pallas_call(
        kernel,
        in_specs=specs,
        out_specs=[VMEM] * len(rows) if len(rows) > 1 else VMEM,
        out_shape=shapes if len(rows) > 1 else shapes[0],
        scratch_shapes=list(scratch),
        input_output_aliases=aliases or {},
        compiler_params=pltpu.CompilerParams(vmem_limit_bytes=32 << 20),
        cost_estimate=pl.CostEstimate(
            flops=int(work * 3e10), bytes_accessed=int(work * COST), transcendentals=0
        ),
        name=name,
    )


def exchange(blocks):
    return lax.all_to_all(
        blocks.reshape(NF, NV, 4, R), "freq", split_axis=0, concat_axis=0, tiled=True
    ).reshape(NF * NC, R)


def group_exchange(blocks, groups):
    return lax.all_to_all(
        blocks, "freq", split_axis=0, concat_axis=0, tiled=True, axis_index_groups=groups
    )


def neighbours(x):
    axes = ("freq", "plane")
    return lax.ppermute(x, axes, TO_PREV), lax.ppermute(x, axes, TO_NEXT)


def swapped(x):
    return lax.ppermute(x, "plane", [(0, 1), (1, 0)])


def edges(planes):
    planes = planes.reshape(NC, AZ, R)
    mine = jnp.concatenate([planes[:, :HALO], planes[:, AZ - HALO :]], axis=1)
    return swapped(mine.reshape(-1, R))


def fetch_planes(ordered, station_index, edge_at):
    held = group_exchange(ordered.reshape(16, 8 * NV, R), FLAT)
    mine = jnp.concatenate(
        [
            lax.dynamic_slice_in_dim(held, station_index[s] // 8, 1, axis=0)
            for s in range(STEPS)
        ],
        axis=0,
    )
    came = group_exchange(
        jnp.broadcast_to(mine.reshape(1, -1, R), (8, STEPS * 8 * NV, R)), TALL
    ).reshape(8, STEPS, 8 * NV, R)
    chosen = [
        lax.dynamic_index_in_dim(came[:, s], station_index[s] % 8, 0, keepdims=False)
        for s in range(STEPS)
    ]
    spread = group_exchange(jnp.broadcast_to(chosen[0][None], (16, 8 * NV, R)), FLAT)
    spread = spread.reshape(AZ * NV, R)
    rim = swapped(
        call(rim_kernel, [SMEM, VMEM], (NV * 2 * HALO,), "rim", 0.1)(edge_at, spread)
    )
    own = lax.dynamic_index_in_dim(
        chosen[1].reshape(8, NV, R), lax.axis_index("freq") % 8, 0, keepdims=False
    )
    return spread, rim, own


def per_device(state_in, forcing_in, base_flow, station_index, lobe_count):
    slopes, inverse_p = radial_tables()
    solve = jnp.asarray(right_factor(inverse_p))
    slope = jnp.asarray(right_factor(slopes))
    inverse, forward = (jnp.asarray(t) for t in transform_tables())
    f = lax.axis_index("freq")
    p = lax.axis_index("plane")

    def of_plane(table):
        return jnp.where(p == 0, jnp.asarray(table[0]), jnp.asarray(table[1]))

    az_of, edge_at = of_plane(AZ_OF), of_plane(EDGE_AT)
    omegas = 0.5 * (f * PER + jnp.arange(PER)).astype(jnp.float32) / FREQS

    def shaped(position):
        phases = lobe_count[0] * position % ALL_AZ
        chevron = 1.0 + 0.5 * jnp.cos(2.0 * math.pi * phases.astype(jnp.float32) / ALL_AZ)
        return BASE_SCALE * chevron

    shape_az = shaped((p * AZ - HALO + jnp.arange(EXT) + ALL_AZ) % ALL_AZ)
    shape_az = jnp.broadcast_to(shape_az[:, None], (EXT, R))

    state = state_in.reshape(NC * AZ, R)
    forcing = forcing_in.reshape(NC * AZ, R)
    ordered = call(sort_kernel, [SMEM, VMEM], (AZ * NV,), "sort", 1)(
        az_of, base_flow.reshape(NV * AZ, R)
    )
    ordered, state, forcing = lax.optimization_barrier((ordered, state, forcing))
    spread, rim, own = fetch_planes(ordered, station_index, edge_at)
    weight = own * shaped(p * AZ + az_of[f])

    send = call(
        march_kernel,
        [SMEM] * 2 + [VMEM] * 8,
        (NC * AZ,),
        "march",
        6,
        (
            pltpu.VMEM((2, NC * EXT + 2 * GUARD, R), jnp.float32),
            pltpu.VMEM((NC * EXT, R), jnp.float32),
            pltpu.VMEM((NV * EXT, R), jnp.float32),
        ),
    )(
        az_of, omegas, state, edges(state), forcing, edges(forcing),
        spread, rim, shape_az, solve,
    )
    counts = [len(vs) for vs in CHUNKS]
    weights = [
        jnp.pad(weight[vs[0] : vs[-1] + 1], ((0, 8 - len(vs)), (0, 0))) for vs in CHUNKS
    ]

    def radial(us):
        return [
            call(
                lambda *refs, first=n == 0: radial_kernel(first, *refs),
                [VMEM] * (2 if n == 0 else 3),
                (counts[n] * NT,),
                "radial",
                0.01,
            )(*((u,) if n == 0 else (us[0], u)), slope)
            for n, u in enumerate(us)
        ]

    unpacked = call(
        unpack_kernel,
        [VMEM] * 2,
        [n * KEPT for n in counts] + [n * NT for n in counts],
        "unpack",
        2,
    )(exchange(send), inverse)
    xs, us = list(unpacked[: len(counts)]), list(unpacked[len(counts) :])
    sides = []
    for n, x in enumerate(xs):
        if sides:
            x, sides[-1] = lax.optimization_barrier((x, sides[-1]))
        sides.append(neighbours(x))
    parts = radial(us)
    bs = []
    before = xs[0]
    for n, x in enumerate(xs):
        xs[n], b = call(
            lambda _, *refs, first=n == 0: forcing_kernel(first, *refs),
            [ANY] + [VMEM] * 9,
            (counts[n] * KEPT,) * 2,
            "forcing",
            counts[n],
            (pltpu.VMEM((NT, R), jnp.float32),) if n == 0 else (),
        )(before, us[0], parts[n], x, *sides[n], weights[n], inverse, forward, solve)
        before = xs[n]
        bs.append(b)
        sides[n] = neighbours(xs[n])
    for sweep in range(1, SWEEPS):
        last = sweep == SWEEPS - 1
        for n, x in enumerate(xs):
            done = call(
                lambda _, *refs: sweep_kernel(*refs),
                [ANY] + [VMEM] * (7 if last else 6),
                (counts[n] * KEPT,) + ((counts[n] * NT,) if last else ()),
                "sweep",
                (0.7 if last else 0.3) * counts[n],
            )(before, x, *sides[n], bs[n], weights[n], solve, *((inverse,) if last else ()))
            if last:
                xs[n], us[n] = done
                sides[n] = neighbours(us[n])
            else:
                xs[n] = done
                sides[n] = neighbours(done)
            before = xs[n]
    packed = call(pack_kernel, [VMEM] * len(xs), (2 * NC * AZ,), "pack", 0.01)(*xs)
    parts = radial(us)
    operands = (
        us[0], *parts, *[s[0] for s in sides], *[s[1] for s in sides], forward, packed
    )
    back = call(
        to_freq_kernel,
        [VMEM] * len(operands),
        (2 * NC * AZ,),
        "to_freq",
        2.5,
        aliases={len(operands) - 1: 0},
    )(*operands)
    got = lax.all_to_all(
        back.reshape(NF, 2 * NC, R), "freq", split_axis=0, concat_axis=0, tiled=True
    ).reshape(-1, R)
    state, forcing = call(place_kernel, [SMEM, VMEM], (NC * AZ,) * 2, "place", 4)(az_of, got)
    return (state.reshape(state_in.shape), forcing.reshape(state_in.shape))


def solution(mesh):
    return jax.shard_map(
        per_device,
        mesh=mesh,
        in_specs=(
            P(None, "freq", None, "plane", None),
            P(None, "freq", None, "plane", None),
            P("freq", None, "plane", None),
            P(),
            P(),
        ),
        out_specs=(P(None, "freq", None, "plane", None), P(None, "freq", None, "plane", None)),
        check_vma=False,
    )
```

time: 301 us -> 276 us (0.917)
  blocking collectives: 176 us -> 121 us
  waiting for transfers between devices: 51.2 us -> 70.8 us
  Pallas kernels: 29.3 us -> 34.2 us
  starting transfers between devices: 31.6 us -> 35.1 us
    all_to_all x4 -> x1, blocking collectives: 176 us -> 43.1 us  [exchange(): lax.all_to_all(blocks.reshape(NF, NV, 4, R), 'freq', split_axis=0, concat...]
    all_to_all x0 -> x1, blocking collectives: none -> 78 us  [per_device(): lax.all_to_all(back.reshape(NF, 2 * NC, R), 'freq', split_axis=0, concat_...]
    ppermute x11 -> x23, waiting for transfers between devices: 33.1 us -> 53 us  [the longest x20 50.6 us: neighbours(): return (lax.ppermute(x, axes, TO_PREV), lax.ppermute(x, axes, TO_NEXT))]
    all_to_all x2 -> x3, starting transfers between devices: 15.1 us -> 20.3 us  [group_exchange(): lax.all_to_all(blocks, 'freq', split_axis=0, concat_axis=0, tiled=True, a...]
    pallas_call x10 -> x19, Pallas kernels: 29.3 us -> 34.2 us  [the longest x2 8.42 us: per_device(): call(lambda _, *refs, first=n == 0: forcing_kernel(first, *refs), [ANY] +...]
    ppermute x11 -> x23, starting transfers between devices: 16.4 us -> 14.8 us  [the longest x20 12.4 us: neighbours(): return (lax.ppermute(x, axes, TO_PREV), lax.ppermute(x, axes, TO_NEXT))]
    all_to_all x2 -> x3, waiting for transfers between devices: 18.1 us -> 17.8 us  [group_exchange(): lax.all_to_all(blocks, 'freq', split_axis=0, concat_axis=0, tiled=True, a...]
  transfers between devices with their start and end apart: 13 -> 26, of which waited for: 10 -> 21; matrix products, arithmetic and copies ran while one was open for 2% -> 2% of each run, Pallas kernels for 0% -> 6%
where the time goes in v2:
time: 276 us; the launch traced here: 275 us
  blocking collectives  121 us (44%)
  waiting for transfers between devices  70.8 us (26%)
  starting transfers between devices  35.1 us (13%)
  Pallas kernels  34.2 us (12%)
  between operations  7.56 us (3%)
  local copies, waits for them, and re-layouts  5.31 us (2%)
    all_to_all x1, blocking collectives, per_device(): lax.all_to_all(back.reshape(NF, 2 * NC, R), 'freq', split_axis=0, concat_...  78 us
    ppermute x20, waiting for transfers between devices, neighbours(): return (lax.ppermute(x, axes, TO_PREV), lax.ppermute(x, axes, TO_NEXT))  50.6 us
    all_to_all x1, blocking collectives, exchange(): lax.all_to_all(blocks.reshape(NF, NV, 4, R), 'freq', split_axis=0, concat...  43.1 us
    all_to_all x3, starting transfers between devices, group_exchange(): lax.all_to_all(blocks, 'freq', split_axis=0, concat_axis=0, tiled=True, a...  20.3 us
    all_to_all x3, waiting for transfers between devices, group_exchange(): lax.all_to_all(blocks, 'freq', split_axis=0, concat_axis=0, tiled=True, a...  17.8 us
    ppermute x20, starting transfers between devices, neighbours(): return (lax.ppermute(x, axes, TO_PREV), lax.ppermute(x, axes, TO_NEXT))  12.4 us
    pallas_call x2, Pallas kernels, per_device(): call(lambda _, *refs, first=n == 0: forcing_kernel(first, *refs), [ANY] +...  8.42 us
    pallas_call x1, Pallas kernels, per_device(): call(march_kernel, [SMEM] * 2 + [VMEM] * 8, (NC * AZ,), 'march', 6, (pltp...  7.17 us
  transfers between devices with their start and end apart: 26, of which 21 were waited for; matrix products, arithmetic and copies ran while one was open for 2% of the time, Pallas kernels for 6%

profile of v2, /device:TPU:33, one launch (start us, length us, event | category | flops | bytes accessed | tf_op | source)
XLA Modules:
  0.0 275.5 jit_solution(4466625416021995599)
XLA Ops:
  3.9 6.9 %all-to-all-start = ((f32[16,40,128]{2,1,0:T(8,128)}), f32[16,40,128]{2,1,0:T(8,128)S(1)}, u32[]{:S(2)}, u32[]{:S(2)}) async-start(f32[16,40,128]{2,1,0:T(8,128)} %bitcast.7), calls=%async_computation | async-start | bytes 655360 | tf_op jit(solution)/shard_map/all_to_all | solution.py:382
  19.4 9.9 %all-to-all-start.1 = ((f32[8,80,128]{2,1,0:T(8,128)}), f32[8,80,128]{2,1,0:T(8,128)S(1)}, u32[]{:S(2)}, u32[]{:S(2)}) async-start(f32[8,80,128]{2,1,0:T(8,128)} %broadcast_in_dim.22), calls=%async_computation.1 | async-start | bytes 655360 | tf_op jit(solution)/shard_map/all_to_all | solution.py:382
  32.2 8.2 %all-to-all-done.1 = f32[8,80,128]{2,1,0:T(8,128)S(1)} async-done(((f32[8,80,128]{2,1,0:T(8,128)}), f32[8,80,128]{2,1,0:T(8,128)S(1)}, u32[]{:S(2)}, u32[]{:S(2)}) %all-to-all-start.1) | async-done | bytes 327712 | tf_op jit(solution)/shard_map/all_to_all | solution.py:382
  41.8 3.6 %all-to-all-start.2 = ((f32[16,40,128]{2,1,0:T(8,128)}), f32[16,40,128]{2,1,0:T(8,128)S(1)}, u32[]{:S(2)}, u32[]{:S(2)}) async-start(f32[16,40,128]{2,1,0:T(8,128)} %broadcast_in_dim.24), calls=%async_computation.2 | async-start | bytes 655360 | tf_op jit(solution)/shard_map/all_to_all | solution.py:382
  45.5 7.6 %all-to-all-done.2 = f32[16,40,128]{2,1,0:T(8,128)S(1)} async-done(((f32[16,40,128]{2,1,0:T(8,128)}), f32[16,40,128]{2,1,0:T(8,128)S(1)}, u32[]{:S(2)}, u32[]{:S(2)}) %all-to-all-start.2) | async-done | bytes 327712 | tf_op jit(solution)/shard_map/all_to_all | solution.py:382
  56.9 7.2 %march.1 = f32[2560,128]{1,0:T(8,128)S(1)} custom-call(s32[128]{0:T(128)S(1)} %broadcast_select_fusion.1.az_ref, f32[2]{0:T(128)S(1)} %convert_multiply_fusion.om_ref, f32[2560,128]{1,0:T(8,128)S(1)} %bitcast.38, f32[320,128]{1,0:T(8,128)S(1)} %collective-permute-done.sedge_ref, f32[2560,128]{1,0:T(8,128)S(1)} %bitcast.40, ...), custom_call_target="tpu_custom_call" | custom-call | flops 179999997952 | bytes 600000000 | tf_op jit(solution)/shard_map/march/pallas_call | solution.py:460
  64.1 43.1 %all_to_all.25 = f32[128,5,4,128]{3,2,1,0:T(4,128)S(1)} all-to-all(f32[128,5,4,128]{3,2,1,0:T(4,128)S(1)} %bitcast.33), channel_id=1, replica_groups=mesh['freq'=128,'plane'=2] {'freq'}, dimensions={0} | all-to-all | bytes 2621440 | tf_op jit(solution)/shard_map/all_to_all | solution.py:376
  109.1 6.5 %collective-permute-start.4 = (f32[1536,128]{1,0:T(8,128)S(1)}, f32[1536,128]{1,0:T(8,128)S(1)}, u32[]{:S(2)}, u32[]{:S(2)}) collective-permute-start(f32[1536,128]{1,0:T(8,128)S(1)} %get-tuple-element.25._.refs_2_), channel_id=1, source_target_pairs={{0,2},{2,64},{64,66},{66,128},{128,130},{130,192},{192,194},{194,2... | collective-permute-start | bytes 2359304 | tf_op jit(solution)/shard_map/ppermute | solution.py:389
  118.4 6.1 %collective-permute-done.4.refs_4_ = f32[1536,128]{1,0:T(8,128)S(1)} collective-permute-done((f32[1536,128]{1,0:T(8,128)S(1)}, f32[1536,128]{1,0:T(8,128)S(1)}, u32[]{:S(2)}, u32[]{:S(2)}) %collective-permute-start.4) | collective-permute-done | bytes 786464 | tf_op jit(solution)/shard_map/ppermute | solution.py:389
  124.6 2.8 %collective-permute-done.3.refs_3_ = f32[1536,128]{1,0:T(8,128)} collective-permute-done((f32[1536,128]{1,0:T(8,128)S(1)}, f32[1536,128]{1,0:T(8,128)}, u32[]{:S(2)}, u32[]{:S(2)}) %collective-permute-start.3) | collective-permute-done | bytes 786464 | tf_op jit(solution)/shard_map/ppermute | solution.py:389
  127.9 5.6 %forcing.2 = (f32[1536,128]{1,0:T(8,128)S(1)}, f32[1536,128]{1,0:T(8,128)S(1)}) custom-call(f32[1536,128]{1,0:T(8,128)S(1)} %get-tuple-element.25._.refs_2_, f32[1152,128]{1,0:T(8,128)S(1)} %get-tuple-element.26.refs_0_, f32[1152,128]{1,0:T(8,128)S(1)} %radial.4.refs_1_, f32[1536,128]{1,0:T(8,128)S(1)} %get-tuple-element.25._.refs_2_, ...), custom_call_target="tpu_custom_call" | custom-call | flops 89999998976 | bytes 300000000 | tf_op jit(solution)/shard_map/forcing/pallas_call | solution.py:509
  136.2 2.8 %forcing.3 = (f32[1024,128]{1,0:T(8,128)S(1)}, f32[1024,128]{1,0:T(8,128)S(1)}) custom-call(f32[1536,128]{1,0:T(8,128)S(1)} %get-tuple-element.30._.refs_0_, f32[1152,128]{1,0:T(8,128)S(1)} %get-tuple-element.26.refs_0_, f32[768,128]{1,0:T(8,128)S(1)} %radial.5.refs_1_, f32[1024,128]{1,0:T(8,128)S(1)} %get-tuple-element.32.refs_2_, ...), custom_call_target="tpu_custom_call" | custom-call | flops 60000002048 | bytes 200000000 | tf_op jit(solution)/shard_map/forcing/pallas_call | solution.py:509
  139.7 4.1 %collective-permute-done.8.refs_2_ = f32[1536,128]{1,0:T(8,128)S(1)} collective-permute-done((f32[1536,128]{1,0:T(8,128)S(1)}, f32[1536,128]{1,0:T(8,128)S(1)}, u32[]{:S(2)}, u32[]{:S(2)}) %collective-permute-start.8) | collective-permute-done | bytes 786464 | tf_op jit(solution)/shard_map/ppermute | solution.py:389
  143.7 2.8 %collective-permute-done.7.refs_1_ = f32[1536,128]{1,0:T(8,128)S(1)} collective-permute-done((f32[1536,128]{1,0:T(8,128)S(1)}, f32[1536,128]{1,0:T(8,128)S(1)}, u32[]{:S(2)}, u32[]{:S(2)}) %collective-permute-start.7) | collective-permute-done | bytes 786464 | tf_op jit(solution)/shard_map/ppermute | solution.py:389
  149.3 2.8 %collective-permute-done.9.refs_1_ = f32[1024,128]{1,0:T(8,128)S(1)} collective-permute-done((f32[1024,128]{1,0:T(8,128)S(1)}, f32[1024,128]{1,0:T(8,128)S(1)}, u32[]{:S(2)}, u32[]{:S(2)}) %collective-permute-start.9) | collective-permute-done | bytes 524320 | tf_op jit(solution)/shard_map/ppermute | solution.py:389
  153.3 4.5 %collective-permute-done.12.refs_2_ = f32[1536,128]{1,0:T(8,128)S(1)} collective-permute-done((f32[1536,128]{1,0:T(8,128)S(1)}, f32[1536,128]{1,0:T(8,128)S(1)}, u32[]{:S(2)}, u32[]{:S(2)}) %collective-permute-start.12) | collective-permute-done | bytes 786464 | tf_op jit(solution)/shard_map/ppermute | solution.py:389
  157.8 2.8 %collective-permute-done.11.refs_1_ = f32[1536,128]{1,0:T(8,128)S(1)} collective-permute-done((f32[1536,128]{1,0:T(8,128)S(1)}, f32[1536,128]{1,0:T(8,128)S(1)}, u32[]{:S(2)}, u32[]{:S(2)}) %collective-permute-start.11) | collective-permute-done | bytes 786464 | tf_op jit(solution)/shard_map/ppermute | solution.py:389
  163.4 2.8 %collective-permute-done.13.refs_1_ = f32[1024,128]{1,0:T(8,128)S(1)} collective-permute-done((f32[1024,128]{1,0:T(8,128)S(1)}, f32[1024,128]{1,0:T(8,128)S(1)}, u32[]{:S(2)}, u32[]{:S(2)}) %collective-permute-start.13) | collective-permute-done | bytes 524320 | tf_op jit(solution)/shard_map/ppermute | solution.py:389
  167.3 4.5 %collective-permute-done.16.refs_2_ = f32[1536,128]{1,0:T(8,128)S(1)} collective-permute-done((f32[1536,128]{1,0:T(8,128)S(1)}, f32[1536,128]{1,0:T(8,128)S(1)}, u32[]{:S(2)}, u32[]{:S(2)}) %collective-permute-start.16) | collective-permute-done | bytes 786464 | tf_op jit(solution)/shard_map/ppermute | solution.py:389
  171.8 2.8 %collective-permute-done.15.refs_1_ = f32[1536,128]{1,0:T(8,128)S(1)} collective-permute-done((f32[1536,128]{1,0:T(8,128)S(1)}, f32[1536,128]{1,0:T(8,128)S(1)}, u32[]{:S(2)}, u32[]{:S(2)}) %collective-permute-start.15) | collective-permute-done | bytes 786464 | tf_op jit(solution)/shard_map/ppermute | solution.py:389
  177.4 2.8 %collective-permute-done.17.refs_1_ = f32[1024,128]{1,0:T(8,128)S(1)} collective-permute-done((f32[1024,128]{1,0:T(8,128)S(1)}, f32[1024,128]{1,0:T(8,128)S(1)}, u32[]{:S(2)}, u32[]{:S(2)}) %collective-permute-start.17) | collective-permute-done | bytes 524320 | tf_op jit(solution)/shard_map/ppermute | solution.py:389
  183.1 4.8 %collective-permute-done.22.refs_6_ = f32[768,128]{1,0:T(8,128)S(1)} collective-permute-done((f32[768,128]{1,0:T(8,128)S(1)}, f32[768,128]{1,0:T(8,128)S(1)}, u32[]{:S(2)}, u32[]{:S(2)}) %collective-permute-start.22) | collective-permute-done | bytes 393248 | tf_op jit(solution)/shard_map/ppermute | solution.py:389
  193.0 78.0 %all_to_all.26 = f32[128,40,128]{2,1,0:T(8,128)S(1)} all-to-all(f32[128,40,128]{2,1,0:T(8,128)S(1)} %bitcast.31), channel_id=1, replica_groups=mesh['freq'=128,'plane'=2] {'freq'}, dimensions={0} | all-to-all | bytes 5242880 | tf_op jit(solution)/shard_map/all_to_all | solution.py:550
  271.0 4.5 %place.1 = (f32[2560,128]{1,0:T(8,128)}, f32[2560,128]{1,0:T(8,128)}) custom-call(s32[128]{0:T(128)S(1)} %broadcast_select_fusion.1.az_ref, f32[5120,128]{1,0:T(8,128)S(1)} %bitcast.32), custom_call_target="tpu_custom_call" | custom-call | flops 120000004096 | bytes 400000000 | tf_op jit(solution)/shard_map/place/pallas_call | solution.py:553
  (99 shorter events, 40.8 us)
Async XLA Ops:
  3.9 14.7 %all-to-all-start = ((f32[16,40,128]{2,1,0:T(8,128)}), f32[16,40,128]{2,1,0:T(8,128)S(1)}, u32[]{:S(2)}, u32[]{:S(2)}) async-start(f32[16,40,128]{2,1,0:T(8,128)} %bitcast.7), calls=%async_computation | async-start | bytes 655360 | tf_op jit(solution)/shard_map/all_to_all | solution.py:382
  19.4 21.0 %all-to-all-start.1 = ((f32[8,80,128]{2,1,0:T(8,128)}), f32[8,80,128]{2,1,0:T(8,128)S(1)}, u32[]{:S(2)}, u32[]{:S(2)}) async-start(f32[8,80,128]{2,1,0:T(8,128)} %broadcast_in_dim.22), calls=%async_computation.1 | async-start | bytes 655360 | tf_op jit(solution)/shard_map/all_to_all | solution.py:382
  29.3 25.1 %collective-permute-start = (f32[320,128]{1,0:T(8,128)S(1)}, f32[320,128]{1,0:T(8,128)S(1)}, u32[]{:S(2)}, u32[]{:S(2)}) collective-permute-start(f32[320,128]{1,0:T(8,128)S(1)} %bitcast.43), channel_id=1, source_target_pairs={{0,1},{1,0},{2,3},{3,2},{4,5},{5,4},{6,7},{7,6},{8,9},{9,8},{10,11... | collective-permute-start | bytes 491528 | tf_op jit(solution)/shard_map/ppermute | solution.py:393
  30.8 23.6 %collective-permute-start.1 = (f32[320,128]{1,0:T(8,128)}, f32[320,128]{1,0:T(8,128)S(1)}, u32[]{:S(2)}, u32[]{:S(2)}) collective-permute-start(f32[320,128]{1,0:T(8,128)} %bitcast.6), channel_id=1, source_target_pairs={{0,1},{1,0},{2,3},{3,2},{4,5},{5,4},{6,7},{7,6},{8,9},{9,8},{10,11... | collective-permute-start | bytes 491528 | tf_op jit(solution)/shard_map/ppermute | solution.py:393
  41.8 11.3 %all-to-all-start.2 = ((f32[16,40,128]{2,1,0:T(8,128)}), f32[16,40,128]{2,1,0:T(8,128)S(1)}, u32[]{:S(2)}, u32[]{:S(2)}) async-start(f32[16,40,128]{2,1,0:T(8,128)} %broadcast_in_dim.24), calls=%async_computation.2 | async-start | bytes 655360 | tf_op jit(solution)/shard_map/all_to_all | solution.py:382
  109.1 15.4 %collective-permute-start.4 = (f32[1536,128]{1,0:T(8,128)S(1)}, f32[1536,128]{1,0:T(8,128)S(1)}, u32[]{:S(2)}, u32[]{:S(2)}) collective-permute-start(f32[1536,128]{1,0:T(8,128)S(1)} %get-tuple-element.25._.refs_2_), channel_id=1, source_target_pairs={{0,2},{2,64},{64,66},{66,128},{128,130},{130,192},{192,194},{194,2... | collective-permute-start | bytes 2359304 | tf_op jit(solution)/shard_map/ppermute | solution.py:389
  115.6 11.7 %collective-permute-start.3 = (f32[1536,128]{1,0:T(8,128)S(1)}, f32[1536,128]{1,0:T(8,128)}, u32[]{:S(2)}, u32[]{:S(2)}) collective-permute-start(f32[1536,128]{1,0:T(8,128)S(1)} %get-tuple-element.25._.refs_2_), channel_id=1, source_target_pairs={{2,0},{64,2},{66,64},{128,66},{130,128},{192,130},{194,192},{208,1... | collective-permute-start | bytes 2359304 | tf_op jit(solution)/shard_map/ppermute | solution.py:389
  127.3 7.5 %collective-permute-start.6 = (f32[1024,128]{1,0:T(8,128)S(1)}, f32[1024,128]{1,0:T(8,128)S(1)}, u32[]{:S(2)}, u32[]{:S(2)}) collective-permute-start(f32[1024,128]{1,0:T(8,128)S(1)} %get-tuple-element.32.refs_2_), channel_id=1, source_target_pairs={{0,2},{2,64},{64,66},{66,128},{128,130},{130,192},{192,194},{194,2... | collective-permute-start | bytes 1572872 | tf_op jit(solution)/shard_map/ppermute | solution.py:389
  127.3 8.9 %collective-permute-start.5 = (f32[1024,128]{1,0:T(8,128)S(1)}, f32[1024,128]{1,0:T(8,128)S(1)}, u32[]{:S(2)}, u32[]{:S(2)}) collective-permute-start(f32[1024,128]{1,0:T(8,128)S(1)} %get-tuple-element.32.refs_2_), channel_id=1, source_target_pairs={{2,0},{64,2},{66,64},{128,66},{130,128},{192,130},{194,192},{208,1... | collective-permute-start | bytes 1572872 | tf_op jit(solution)/shard_map/ppermute | solution.py:389
  133.5 10.3 %collective-permute-start.8 = (f32[1536,128]{1,0:T(8,128)S(1)}, f32[1536,128]{1,0:T(8,128)S(1)}, u32[]{:S(2)}, u32[]{:S(2)}) collective-permute-start(f32[1536,128]{1,0:T(8,128)S(1)} %get-tuple-element.30._.refs_0_), channel_id=1, source_target_pairs={{0,2},{2,64},{64,66},{66,128},{128,130},{130,192},{192,194},{194,2... | collective-permute-start | bytes 2359304 | tf_op jit(solution)/shard_map/ppermute | solution.py:389
  134.8 11.7 %collective-permute-start.7 = (f32[1536,128]{1,0:T(8,128)S(1)}, f32[1536,128]{1,0:T(8,128)S(1)}, u32[]{:S(2)}, u32[]{:S(2)}) collective-permute-start(f32[1536,128]{1,0:T(8,128)S(1)} %get-tuple-element.30._.refs_0_), channel_id=1, source_target_pairs={{2,0},{64,2},{66,64},{128,66},{130,128},{192,130},{194,192},{208,1... | collective-permute-start | bytes 2359304 | tf_op jit(solution)/shard_map/ppermute | solution.py:389
  139.1 10.3 %collective-permute-start.10 = (f32[1024,128]{1,0:T(8,128)S(1)}, f32[1024,128]{1,0:T(8,128)S(1)}, u32[]{:S(2)}, u32[]{:S(2)}) collective-permute-start(f32[1024,128]{1,0:T(8,128)S(1)} %get-tuple-element.33._.refs_0_), channel_id=1, source_target_pairs={{0,2},{2,64},{64,66},{66,128},{128,130},{130,192},{192,194},{194,2... | collective-permute-start | bytes 1572872 | tf_op jit(solution)/shard_map/ppermute | solution.py:389
  139.4 12.7 %collective-permute-start.9 = (f32[1024,128]{1,0:T(8,128)S(1)}, f32[1024,128]{1,0:T(8,128)S(1)}, u32[]{:S(2)}, u32[]{:S(2)}) collective-permute-start(f32[1024,128]{1,0:T(8,128)S(1)} %get-tuple-element.33._.refs_0_), channel_id=1, source_target_pairs={{2,0},{64,2},{66,64},{128,66},{130,128},{192,130},{194,192},{208,1... | collective-permute-start | bytes 1572872 | tf_op jit(solution)/shard_map/ppermute | solution.py:389
  147.3 10.5 %collective-permute-start.12 = (f32[1536,128]{1,0:T(8,128)S(1)}, f32[1536,128]{1,0:T(8,128)S(1)}, u32[]{:S(2)}, u32[]{:S(2)}) collective-permute-start(f32[1536,128]{1,0:T(8,128)S(1)} %sweep.6._.refs_0_), channel_id=1, source_target_pairs={{0,2},{2,64},{64,66},{66,128},{128,130},{130,192},{192,194},{194,2... | collective-permute-start | bytes 2359304 | tf_op jit(solution)/shard_map/ppermute | solution.py:389
  147.4 13.2 %collective-permute-start.11 = (f32[1536,128]{1,0:T(8,128)S(1)}, f32[1536,128]{1,0:T(8,128)S(1)}, u32[]{:S(2)}, u32[]{:S(2)}) collective-permute-start(f32[1536,128]{1,0:T(8,128)S(1)} %sweep.6._.refs_0_), channel_id=1, source_target_pairs={{2,0},{64,2},{66,64},{128,66},{130,128},{192,130},{194,192},{208,1... | collective-permute-start | bytes 2359304 | tf_op jit(solution)/shard_map/ppermute | solution.py:389
  152.7 10.7 %collective-permute-start.14 = (f32[1024,128]{1,0:T(8,128)S(1)}, f32[1024,128]{1,0:T(8,128)S(1)}, u32[]{:S(2)}, u32[]{:S(2)}) collective-permute-start(f32[1024,128]{1,0:T(8,128)S(1)} %sweep.7._.refs_0_), channel_id=1, source_target_pairs={{0,2},{2,64},{64,66},{66,128},{128,130},{130,192},{192,194},{194,2... | collective-permute-start | bytes 1572872 | tf_op jit(solution)/shard_map/ppermute | solution.py:389
  152.8 13.4 %collective-permute-start.13 = (f32[1024,128]{1,0:T(8,128)S(1)}, f32[1024,128]{1,0:T(8,128)S(1)}, u32[]{:S(2)}, u32[]{:S(2)}) collective-permute-start(f32[1024,128]{1,0:T(8,128)S(1)} %sweep.7._.refs_0_), channel_id=1, source_target_pairs={{2,0},{64,2},{66,64},{128,66},{130,128},{192,130},{194,192},{208,1... | collective-permute-start | bytes 1572872 | tf_op jit(solution)/shard_map/ppermute | solution.py:389
  161.3 10.5 %collective-permute-start.16 = (f32[1536,128]{1,0:T(8,128)S(1)}, f32[1536,128]{1,0:T(8,128)S(1)}, u32[]{:S(2)}, u32[]{:S(2)}) collective-permute-start(f32[1536,128]{1,0:T(8,128)S(1)} %sweep.8._.refs_0_), channel_id=1, source_target_pairs={{0,2},{2,64},{64,66},{66,128},{128,130},{130,192},{192,194},{194,2... | collective-permute-start | bytes 2359304 | tf_op jit(solution)/shard_map/ppermute | solution.py:389
  161.4 13.2 %collective-permute-start.15 = (f32[1536,128]{1,0:T(8,128)S(1)}, f32[1536,128]{1,0:T(8,128)S(1)}, u32[]{:S(2)}, u32[]{:S(2)}) collective-permute-start(f32[1536,128]{1,0:T(8,128)S(1)} %sweep.8._.refs_0_), channel_id=1, source_target_pairs={{2,0},{64,2},{66,64},{128,66},{130,128},{192,130},{194,192},{208,1... | collective-permute-start | bytes 2359304 | tf_op jit(solution)/shard_map/ppermute | solution.py:389
  166.7 10.7 %collective-permute-start.18 = (f32[1024,128]{1,0:T(8,128)S(1)}, f32[1024,128]{1,0:T(8,128)S(1)}, u32[]{:S(2)}, u32[]{:S(2)}) collective-permute-start(f32[1024,128]{1,0:T(8,128)S(1)} %sweep.9._.refs_0_), channel_id=1, source_target_pairs={{0,2},{2,64},{64,66},{66,128},{128,130},{130,192},{192,194},{194,2... | collective-permute-start | bytes 1572872 | tf_op jit(solution)/shard_map/ppermute | solution.py:389
  166.8 13.4 %collective-permute-start.17 = (f32[1024,128]{1,0:T(8,128)S(1)}, f32[1024,128]{1,0:T(8,128)S(1)}, u32[]{:S(2)}, u32[]{:S(2)}) collective-permute-start(f32[1024,128]{1,0:T(8,128)S(1)} %sweep.9._.refs_0_), channel_id=1, source_target_pairs={{2,0},{64,2},{66,64},{128,66},{130,128},{192,130},{194,192},{208,1... | collective-permute-start | bytes 1572872 | tf_op jit(solution)/shard_map/ppermute | solution.py:389
  176.6 13.9 %collective-permute-start.21 = (f32[1152,128]{1,0:T(8,128)S(1)}, f32[1152,128]{1,0:T(8,128)S(1)}, u32[]{:S(2)}, u32[]{:S(2)}) collective-permute-start(f32[1152,128]{1,0:T(8,128)S(1)} %get-tuple-element.36.refs_0_), channel_id=1, source_target_pairs={{0,2},{2,64},{64,66},{66,128},{128,130},{130,192},{192,194},{194,2... | collective-permute-start | bytes 1769480 | tf_op jit(solution)/shard_map/ppermute | solution.py:389
  176.7 13.8 %collective-permute-start.19 = (f32[1152,128]{1,0:T(8,128)S(1)}, f32[1152,128]{1,0:T(8,128)S(1)}, u32[]{:S(2)}, u32[]{:S(2)}) collective-permute-start(f32[1152,128]{1,0:T(8,128)S(1)} %get-tuple-element.36.refs_0_), channel_id=1, source_target_pairs={{2,0},{64,2},{66,64},{128,66},{130,128},{192,130},{194,192},{208,1... | collective-permute-start | bytes 1769480 | tf_op jit(solution)/shard_map/ppermute | solution.py:389
  181.6 8.8 %collective-permute-start.20 = (f32[768,128]{1,0:T(8,128)S(1)}, f32[768,128]{1,0:T(8,128)S(1)}, u32[]{:S(2)}, u32[]{:S(2)}) collective-permute-start(f32[768,128]{1,0:T(8,128)S(1)} %get-tuple-element.38.refs_1_), channel_id=1, source_target_pairs={{2,0},{64,2},{66,64},{128,66},{130,128},{192,130},{194,192},{208,1... | collective-permute-start | bytes 1179656 | tf_op jit(solution)/shard_map/ppermute | solution.py:389
  (15 other events, 200.0 us)

commit v3 on v2

--- a/solution.py
+++ b/solution.py
@@ -26,7 +26,7 @@
 FREQS = NF * PER
 NT = 3 * FREQS // 2
 NC = 2 * PER * NV
-HALO = 8
+HALO = 4
 EXT = AZ + 2 * HALO
 GUARD = 8
 KEPT = 2 * FREQS
@@ -364,7 +364,7 @@
         out_shape=shapes if len(rows) > 1 else shapes[0],
         scratch_shapes=list(scratch),
         input_output_aliases=aliases or {},
-        compiler_params=pltpu.CompilerParams(vmem_limit_bytes=32 << 20),
+        compiler_params=pltpu.CompilerParams(vmem_limit_bytes=16 << 20),
         cost_estimate=pl.CostEstimate(
             flops=int(work * 3e10), bytes_accessed=int(work * COST), transcendentals=0
         ),
@@ -399,31 +399,31 @@
     return swapped(mine.reshape(-1, R))
 
 
-def fetch_planes(ordered, station_index, edge_at):
+def fetch_planes(ordered, station_index, edge_at, state, forcing):
     held = group_exchange(ordered.reshape(16, 8 * NV, R), FLAT)
-    mine = jnp.concatenate(
-        [
-            lax.dynamic_slice_in_dim(held, station_index[s] // 8, 1, axis=0)
-            for s in range(STEPS)
-        ],
-        axis=0,
-    )
-    came = group_exchange(
-        jnp.broadcast_to(mine.reshape(1, -1, R), (8, STEPS * 8 * NV, R)), TALL
-    ).reshape(8, STEPS, 8 * NV, R)
-    chosen = [
-        lax.dynamic_index_in_dim(came[:, s], station_index[s] % 8, 0, keepdims=False)
+    mine = [
+        lax.dynamic_index_in_dim(held, station_index[s] // 8, 0, keepdims=False)
         for s in range(STEPS)
     ]
-    spread = group_exchange(jnp.broadcast_to(chosen[0][None], (16, 8 * NV, R)), FLAT)
-    spread = spread.reshape(AZ * NV, R)
+    block = jnp.concatenate(
+        [
+            jnp.broadcast_to(mine[0][None], (8, 8 * NV, R)),
+            jnp.pad(mine[1].reshape(8, NV, R), ((0, 0), (0, 3), (0, 0))),
+        ],
+        axis=1,
+    )
+    came = group_exchange(block, TALL)
+    came, state, forcing = lax.optimization_barrier((came, state, forcing))
+    beside = edges(state), edges(forcing)
+    chosen = lax.dynamic_index_in_dim(came, station_index[0] % 8, 0, keepdims=False)
+    own = lax.dynamic_index_in_dim(came, station_index[1] % 8, 0, keepdims=False)
+    spread = group_exchange(
+        jnp.broadcast_to(chosen[None, : 8 * NV], (16, 8 * NV, R)), FLAT
+    ).reshape(AZ * NV, R)
     rim = swapped(
         call(rim_kernel, [SMEM, VMEM], (NV * 2 * HALO,), "rim", 0.1)(edge_at, spread)
     )
-    own = lax.dynamic_index_in_dim(
-        chosen[1].reshape(8, NV, R), lax.axis_index("freq") % 8, 0, keepdims=False
-    )
-    return spread, rim, own
+    return spread, rim, own[8 * NV : 9 * NV], beside
 
 
 def per_device(state_in, forcing_in, base_flow, station_index, lobe_count):
@@ -453,8 +453,7 @@
     ordered = call(sort_kernel, [SMEM, VMEM], (AZ * NV,), "sort", 1)(
         az_of, base_flow.reshape(NV * AZ, R)
     )
-    ordered, state, forcing = lax.optimization_barrier((ordered, state, forcing))
-    spread, rim, own = fetch_planes(ordered, station_index, edge_at)
+    spread, rim, own, beside = fetch_planes(ordered, station_index, edge_at, state, forcing)
     weight = own * shaped(p * AZ + az_of[f])
 
     send = call(
@@ -469,7 +468,7 @@
             pltpu.VMEM((NV * EXT, R), jnp.float32),
         ),
     )(
-        az_of, omegas, state, edges(state), forcing, edges(forcing),
+        az_of, omegas, state, beside[0], forcing, beside[1],
         spread, rim, shape_az, solve,
     )
     counts = [len(vs) for vs in CHUNKS]

time: 276 us -> 273 us (0.989)
  blocking collectives: 121 us -> 126 us
  starting transfers between devices: 35.1 us -> 30.9 us
    all_to_all x1, blocking collectives: 43.1 us -> 48 us  [exchange(): lax.all_to_all(blocks.reshape(NF, NV, 4, R), 'freq', split_axis=0, concat...]
    ppermute x20, starting transfers between devices: 12.4 us -> 7.68 us  [neighbours(): return (lax.ppermute(x, axes, TO_PREV), lax.ppermute(x, axes, TO_NEXT))]
  transfers between devices with their start and end apart: 26 -> 26, of which waited for: 21 -> 21; matrix products, arithmetic and copies ran while one was open for 2% -> 1% of each run, Pallas kernels for 6% -> 6%
where the time goes in v3:
time: 273 us; the launch traced here: 272 us
  blocking collectives  126 us (46%)
  waiting for transfers between devices  68.7 us (25%)
  Pallas kernels  33.2 us (12%)
  starting transfers between devices  30.9 us (11%)
  between operations  7.55 us (3%)
  local copies, waits for them, and re-layouts  3.16 us (1%)
    all_to_all x1, blocking collectives, per_device(): lax.all_to_all(back.reshape(NF, 2 * NC, R), 'freq', split_axis=0, concat_...  78.2 us
    ppermute x20, waiting for transfers between devices, neighbours(): return (lax.ppermute(x, axes, TO_PREV), lax.ppermute(x, axes, TO_NEXT))  50.3 us
    all_to_all x1, blocking collectives, exchange(): lax.all_to_all(blocks.reshape(NF, NV, 4, R), 'freq', split_axis=0, concat...  48 us
    all_to_all x3, starting transfers between devices, group_exchange(): lax.all_to_all(blocks, 'freq', split_axis=0, concat_axis=0, tiled=True, a...  20.3 us
    all_to_all x3, waiting for transfers between devices, group_exchange(): lax.all_to_all(blocks, 'freq', split_axis=0, concat_axis=0, tiled=True, a...  16.8 us
    pallas_call x2, Pallas kernels, per_device(): call(lambda _, *refs, first=n == 0: forcing_kernel(first, *refs), [ANY] +...  8.38 us
    ppermute x20, starting transfers between devices, neighbours(): return (lax.ppermute(x, axes, TO_PREV), lax.ppermute(x, axes, TO_NEXT))  7.68 us
    pallas_call x1, Pallas kernels, per_device(): call(march_kernel, [SMEM] * 2 + [VMEM] * 8, (NC * AZ,), 'march', 6, (pltp...  6.15 us
  transfers between devices with their start and end apart: 26, of which 21 were waited for; matrix products, arithmetic and copies ran while one was open for 1% of the time, Pallas kernels for 6%

profile of v3, /device:TPU:33, one launch (start us, length us, event | category | flops | bytes accessed | tf_op | source)
XLA Modules:
  0.0 271.9 jit_solution(15714244601644124557)
XLA Ops:
  3.9 6.9 %all-to-all-start = ((f32[16,40,128]{2,1,0:T(8,128)}), f32[16,40,128]{2,1,0:T(8,128)S(1)}, u32[]{:S(2)}, u32[]{:S(2)}) async-start(f32[16,40,128]{2,1,0:T(8,128)} %bitcast.2), calls=%async_computation | async-start | bytes 655360 | tf_op jit(solution)/shard_map/all_to_all | solution.py:382
  19.3 9.9 %all-to-all-start.1 = ((f32[8,48,128]{2,1,0:T(8,128)}), f32[8,48,128]{2,1,0:T(8,128)S(1)}, u32[]{:S(2)}, u32[]{:S(2)}) async-start(f32[8,48,128]{2,1,0:T(8,128)} %select_maximum_fusion), calls=%async_computation.1 | async-start | bytes 393216 | tf_op jit(solution)/shard_map/all_to_all | solution.py:382
  29.9 8.5 %all-to-all-done.1 = f32[8,48,128]{2,1,0:T(8,128)S(1)} async-done(((f32[8,48,128]{2,1,0:T(8,128)}), f32[8,48,128]{2,1,0:T(8,128)S(1)}, u32[]{:S(2)}, u32[]{:S(2)}) %all-to-all-start.1) | async-done | bytes 196640 | tf_op jit(solution)/shard_map/all_to_all | solution.py:382
  39.5 3.6 %all-to-all-start.2 = ((f32[16,40,128]{2,1,0:T(8,128)}), f32[16,40,128]{2,1,0:T(8,128)S(1)}, u32[]{:S(2)}, u32[]{:S(2)}) async-start(f32[16,40,128]{2,1,0:T(8,128)} %broadcast_in_dim.25), calls=%async_computation.2 | async-start | bytes 655360 | tf_op jit(solution)/shard_map/all_to_all | solution.py:382
  44.5 6.3 %all-to-all-done.2 = f32[16,40,128]{2,1,0:T(8,128)S(1)} async-done(((f32[16,40,128]{2,1,0:T(8,128)}), f32[16,40,128]{2,1,0:T(8,128)S(1)}, u32[]{:S(2)}, u32[]{:S(2)}) %all-to-all-start.2) | async-done | bytes 327712 | tf_op jit(solution)/shard_map/all_to_all | solution.py:382
  54.3 6.2 %march.1 = f32[2560,128]{1,0:T(8,128)S(1)} custom-call(s32[128]{0:T(128)S(1)} %broadcast_select_fusion.1.az_ref, f32[2]{0:T(128)S(1)} %convert_multiply_fusion.om_ref, f32[2560,128]{1,0:T(8,128)S(1)} %bitcast.38, f32[160,128]{1,0:T(8,128)S(1)} %collective-permute-done.sedge_ref, f32[2560,128]{1,0:T(8,128)S(1)} %bitcast.40, ...), custom_call_target="tpu_custom_call" | custom-call | flops 179999997952 | bytes 600000000 | tf_op jit(solution)/shard_map/march/pallas_call | solution.py:459
  60.5 48.0 %all_to_all.25 = f32[128,5,4,128]{3,2,1,0:T(4,128)S(1)} all-to-all(f32[128,5,4,128]{3,2,1,0:T(4,128)S(1)} %bitcast.33), channel_id=1, replica_groups=mesh['freq'=128,'plane'=2] {'freq'}, dimensions={0} | all-to-all | bytes 2621440 | tf_op jit(solution)/shard_map/all_to_all | solution.py:376
  114.9 6.2 %collective-permute-done.4.refs_4_ = f32[1536,128]{1,0:T(8,128)S(1)} collective-permute-done((f32[1536,128]{1,0:T(8,128)S(1)}, f32[1536,128]{1,0:T(8,128)S(1)}, u32[]{:S(2)}, u32[]{:S(2)}) %collective-permute-start.4) | collective-permute-done | bytes 786464 | tf_op jit(solution)/shard_map/ppermute | solution.py:389
  121.1 2.6 collective-permute-done.3.refs_3_
  124.2 5.6 %forcing.2 = (f32[1536,128]{1,0:T(8,128)S(1)}, f32[1536,128]{1,0:T(8,128)S(1)}) custom-call(f32[1536,128]{1,0:T(8,128)S(1)} %get-tuple-element.25._.refs_2_, f32[1152,128]{1,0:T(8,128)S(1)} %get-tuple-element.26.refs_0_, f32[1152,128]{1,0:T(8,128)S(1)} %radial.4.refs_1_, f32[1536,128]{1,0:T(8,128)S(1)} %get-tuple-element.25._.refs_2_, ...), custom_call_target="tpu_custom_call" | custom-call | flops 89999998976 | bytes 300000000 | tf_op jit(solution)/shard_map/forcing/pallas_call | solution.py:508
  132.3 2.8 %forcing.3 = (f32[1024,128]{1,0:T(8,128)S(1)}, f32[1024,128]{1,0:T(8,128)S(1)}) custom-call(f32[1536,128]{1,0:T(8,128)S(1)} %get-tuple-element.30._.refs_0_, f32[1152,128]{1,0:T(8,128)S(1)} %get-tuple-element.26.refs_0_, f32[768,128]{1,0:T(8,128)S(1)} %radial.5.refs_1_, f32[1024,128]{1,0:T(8,128)S(1)} %get-tuple-element.32.refs_2_, ...), custom_call_target="tpu_custom_call" | custom-call | flops 60000002048 | bytes 200000000 | tf_op jit(solution)/shard_map/forcing/pallas_call | solution.py:508
  135.7 4.3 %collective-permute-done.8.refs_2_ = f32[1536,128]{1,0:T(8,128)S(1)} collective-permute-done((f32[1536,128]{1,0:T(8,128)S(1)}, f32[1536,128]{1,0:T(8,128)S(1)}, u32[]{:S(2)}, u32[]{:S(2)}) %collective-permute-start.8) | collective-permute-done | bytes 786464 | tf_op jit(solution)/shard_map/ppermute | solution.py:389
  140.0 2.8 %collective-permute-done.7.refs_1_ = f32[1536,128]{1,0:T(8,128)S(1)} collective-permute-done((f32[1536,128]{1,0:T(8,128)S(1)}, f32[1536,128]{1,0:T(8,128)S(1)}, u32[]{:S(2)}, u32[]{:S(2)}) %collective-permute-start.7) | collective-permute-done | bytes 786464 | tf_op jit(solution)/shard_map/ppermute | solution.py:389
  145.6 2.8 %collective-permute-done.9.refs_1_ = f32[1024,128]{1,0:T(8,128)S(1)} collective-permute-done((f32[1024,128]{1,0:T(8,128)S(1)}, f32[1024,128]{1,0:T(8,128)S(1)}, u32[]{:S(2)}, u32[]{:S(2)}) %collective-permute-start.9) | collective-permute-done | bytes 524320 | tf_op jit(solution)/shard_map/ppermute | solution.py:389
  149.6 4.5 %collective-permute-done.12.refs_2_ = f32[1536,128]{1,0:T(8,128)S(1)} collective-permute-done((f32[1536,128]{1,0:T(8,128)S(1)}, f32[1536,128]{1,0:T(8,128)S(1)}, u32[]{:S(2)}, u32[]{:S(2)}) %collective-permute-start.12) | collective-permute-done | bytes 786464 | tf_op jit(solution)/shard_map/ppermute | solution.py:389
  154.1 2.8 %collective-permute-done.11.refs_1_ = f32[1536,128]{1,0:T(8,128)S(1)} collective-permute-done((f32[1536,128]{1,0:T(8,128)S(1)}, f32[1536,128]{1,0:T(8,128)S(1)}, u32[]{:S(2)}, u32[]{:S(2)}) %collective-permute-start.11) | collective-permute-done | bytes 786464 | tf_op jit(solution)/shard_map/ppermute | solution.py:389
  159.7 2.8 %collective-permute-done.13.refs_1_ = f32[1024,128]{1,0:T(8,128)S(1)} collective-permute-done((f32[1024,128]{1,0:T(8,128)S(1)}, f32[1024,128]{1,0:T(8,128)S(1)}, u32[]{:S(2)}, u32[]{:S(2)}) %collective-permute-start.13) | collective-permute-done | bytes 524320 | tf_op jit(solution)/shard_map/ppermute | solution.py:389
  163.6 4.5 %collective-permute-done.16.refs_2_ = f32[1536,128]{1,0:T(8,128)S(1)} collective-permute-done((f32[1536,128]{1,0:T(8,128)S(1)}, f32[1536,128]{1,0:T(8,128)S(1)}, u32[]{:S(2)}, u32[]{:S(2)}) %collective-permute-start.16) | collective-permute-done | bytes 786464 | tf_op jit(solution)/shard_map/ppermute | solution.py:389
  168.1 2.8 %collective-permute-done.15.refs_1_ = f32[1536,128]{1,0:T(8,128)S(1)} collective-permute-done((f32[1536,128]{1,0:T(8,128)S(1)}, f32[1536,128]{1,0:T(8,128)S(1)}, u32[]{:S(2)}, u32[]{:S(2)}) %collective-permute-start.15) | collective-permute-done | bytes 786464 | tf_op jit(solution)/shard_map/ppermute | solution.py:389
  173.7 2.8 %collective-permute-done.17.refs_1_ = f32[1024,128]{1,0:T(8,128)S(1)} collective-permute-done((f32[1024,128]{1,0:T(8,128)S(1)}, f32[1024,128]{1,0:T(8,128)S(1)}, u32[]{:S(2)}, u32[]{:S(2)}) %collective-permute-start.17) | collective-permute-done | bytes 524320 | tf_op jit(solution)/shard_map/ppermute | solution.py:389
  179.4 4.8 %collective-permute-done.22.refs_6_ = f32[768,128]{1,0:T(8,128)S(1)} collective-permute-done((f32[768,128]{1,0:T(8,128)S(1)}, f32[768,128]{1,0:T(8,128)S(1)}, u32[]{:S(2)}, u32[]{:S(2)}) %collective-permute-start.22) | collective-permute-done | bytes 393248 | tf_op jit(solution)/shard_map/ppermute | solution.py:389
  184.3 2.5 collective-permute-done.20.refs_4_
  189.2 78.2 %all_to_all.26 = f32[128,40,128]{2,1,0:T(8,128)S(1)} all-to-all(f32[128,40,128]{2,1,0:T(8,128)S(1)} %bitcast.31), channel_id=1, replica_groups=mesh['freq'=128,'plane'=2] {'freq'}, dimensions={0} | all-to-all | bytes 5242880 | tf_op jit(solution)/shard_map/all_to_all | solution.py:549
  267.4 4.5 %place.1 = (f32[2560,128]{1,0:T(8,128)}, f32[2560,128]{1,0:T(8,128)}) custom-call(s32[128]{0:T(128)S(1)} %broadcast_select_fusion.1.az_ref, f32[5120,128]{1,0:T(8,128)S(1)} %bitcast.32), custom_call_target="tpu_custom_call" | custom-call | flops 120000004096 | bytes 400000000 | tf_op jit(solution)/shard_map/place/pallas_call | solution.py:552
  (99 shorter events, 38.0 us)
Async XLA Ops:
  3.9 14.7 %all-to-all-start = ((f32[16,40,128]{2,1,0:T(8,128)}), f32[16,40,128]{2,1,0:T(8,128)S(1)}, u32[]{:S(2)}, u32[]{:S(2)}) async-start(f32[16,40,128]{2,1,0:T(8,128)} %bitcast.2), calls=%async_computation | async-start | bytes 655360 | tf_op jit(solution)/shard_map/all_to_all | solution.py:382
  19.3 19.1 %all-to-all-start.1 = ((f32[8,48,128]{2,1,0:T(8,128)}), f32[8,48,128]{2,1,0:T(8,128)S(1)}, u32[]{:S(2)}, u32[]{:S(2)}) async-start(f32[8,48,128]{2,1,0:T(8,128)} %select_maximum_fusion), calls=%async_computation.1 | async-start | bytes 393216 | tf_op jit(solution)/shard_map/all_to_all | solution.py:382
  38.5 14.2 %collective-permute-start = (f32[160,128]{1,0:T(8,128)S(1)}, f32[160,128]{1,0:T(8,128)S(1)}, u32[]{:S(2)}, u32[]{:S(2)}) collective-permute-start(f32[160,128]{1,0:T(8,128)S(1)} %maximum_bitcast_fusion), channel_id=1, source_target_pairs={{0,1},{1,0},{2,3},{3,2},{4,5},{5,4},{6,7},{7,6},{8,9},{9,8},{10,11... | collective-permute-start | bytes 245768 | tf_op jit(solution)/shard_map/ppermute | solution.py:393
  39.5 11.4 %all-to-all-start.2 = ((f32[16,40,128]{2,1,0:T(8,128)}), f32[16,40,128]{2,1,0:T(8,128)S(1)}, u32[]{:S(2)}, u32[]{:S(2)}) async-start(f32[16,40,128]{2,1,0:T(8,128)} %broadcast_in_dim.25), calls=%async_computation.2 | async-start | bytes 655360 | tf_op jit(solution)/shard_map/all_to_all | solution.py:382
  43.1 9.6 %collective-permute-start.1 = (f32[160,128]{1,0:T(8,128)S(1)}, f32[160,128]{1,0:T(8,128)S(1)}, u32[]{:S(2)}, u32[]{:S(2)}) collective-permute-start(f32[160,128]{1,0:T(8,128)S(1)} %maximum_bitcast_fusion.1), channel_id=1, source_target_pairs={{0,1},{1,0},{2,3},{3,2},{4,5},{5,4},{6,7},{7,6},{8,9},{9,8},{10,11... | collective-permute-start | bytes 245768 | tf_op jit(solution)/shard_map/ppermute | solution.py:393
  110.4 10.7 %collective-permute-start.4 = (f32[1536,128]{1,0:T(8,128)S(1)}, f32[1536,128]{1,0:T(8,128)S(1)}, u32[]{:S(2)}, u32[]{:S(2)}) collective-permute-start(f32[1536,128]{1,0:T(8,128)S(1)} %get-tuple-element.25._.refs_2_), channel_id=1, source_target_pairs={{0,2},{2,64},{64,66},{66,128},{128,130},{130,192},{192,194},{194,2... | collective-permute-start | bytes 2359304 | tf_op jit(solution)/shard_map/ppermute | solution.py:389
  112.1 11.5 %collective-permute-start.3 = (f32[1536,128]{1,0:T(8,128)S(1)}, f32[1536,128]{1,0:T(8,128)}, u32[]{:S(2)}, u32[]{:S(2)}) collective-permute-start(f32[1536,128]{1,0:T(8,128)S(1)} %get-tuple-element.25._.refs_2_), channel_id=1, source_target_pairs={{2,0},{64,2},{66,64},{128,66},{130,128},{192,130},{194,192},{208,1... | collective-permute-start | bytes 2359304 | tf_op jit(solution)/shard_map/ppermute | solution.py:389
  123.7 7.4 %collective-permute-start.6 = (f32[1024,128]{1,0:T(8,128)S(1)}, f32[1024,128]{1,0:T(8,128)S(1)}, u32[]{:S(2)}, u32[]{:S(2)}) collective-permute-start(f32[1024,128]{1,0:T(8,128)S(1)} %get-tuple-element.32.refs_2_), channel_id=1, source_target_pairs={{0,2},{2,64},{64,66},{66,128},{128,130},{130,192},{192,194},{194,2... | collective-permute-start | bytes 1572872 | tf_op jit(solution)/shard_map/ppermute | solution.py:389
  123.7 8.6 %collective-permute-start.5 = (f32[1024,128]{1,0:T(8,128)S(1)}, f32[1024,128]{1,0:T(8,128)S(1)}, u32[]{:S(2)}, u32[]{:S(2)}) collective-permute-start(f32[1024,128]{1,0:T(8,128)S(1)} %get-tuple-element.32.refs_2_), channel_id=1, source_target_pairs={{2,0},{64,2},{66,64},{128,66},{130,128},{192,130},{194,192},{208,1... | collective-permute-start | bytes 1572872 | tf_op jit(solution)/shard_map/ppermute | solution.py:389
  129.8 10.3 %collective-permute-start.8 = (f32[1536,128]{1,0:T(8,128)S(1)}, f32[1536,128]{1,0:T(8,128)S(1)}, u32[]{:S(2)}, u32[]{:S(2)}) collective-permute-start(f32[1536,128]{1,0:T(8,128)S(1)} %get-tuple-element.30._.refs_0_), channel_id=1, source_target_pairs={{0,2},{2,64},{64,66},{66,128},{128,130},{130,192},{192,194},{194,2... | collective-permute-start | bytes 2359304 | tf_op jit(solution)/shard_map/ppermute | solution.py:389
  131.1 11.7 %collective-permute-start.7 = (f32[1536,128]{1,0:T(8,128)S(1)}, f32[1536,128]{1,0:T(8,128)S(1)}, u32[]{:S(2)}, u32[]{:S(2)}) collective-permute-start(f32[1536,128]{1,0:T(8,128)S(1)} %get-tuple-element.30._.refs_0_), channel_id=1, source_target_pairs={{2,0},{64,2},{66,64},{128,66},{130,128},{192,130},{194,192},{208,1... | collective-permute-start | bytes 2359304 | tf_op jit(solution)/shard_map/ppermute | solution.py:389
  135.1 10.5 %collective-permute-start.10 = (f32[1024,128]{1,0:T(8,128)S(1)}, f32[1024,128]{1,0:T(8,128)S(1)}, u32[]{:S(2)}, u32[]{:S(2)}) collective-permute-start(f32[1024,128]{1,0:T(8,128)S(1)} %get-tuple-element.33._.refs_0_), channel_id=1, source_target_pairs={{0,2},{2,64},{64,66},{66,128},{128,130},{130,192},{192,194},{194,2... | collective-permute-start | bytes 1572872 | tf_op jit(solution)/shard_map/ppermute | solution.py:389
  135.7 12.7 %collective-permute-start.9 = (f32[1024,128]{1,0:T(8,128)S(1)}, f32[1024,128]{1,0:T(8,128)S(1)}, u32[]{:S(2)}, u32[]{:S(2)}) collective-permute-start(f32[1024,128]{1,0:T(8,128)S(1)} %get-tuple-element.33._.refs_0_), channel_id=1, source_target_pairs={{2,0},{64,2},{66,64},{128,66},{130,128},{192,130},{194,192},{208,1... | collective-permute-start | bytes 1572872 | tf_op jit(solution)/shard_map/ppermute | solution.py:389
  143.6 10.5 %collective-permute-start.12 = (f32[1536,128]{1,0:T(8,128)S(1)}, f32[1536,128]{1,0:T(8,128)S(1)}, u32[]{:S(2)}, u32[]{:S(2)}) collective-permute-start(f32[1536,128]{1,0:T(8,128)S(1)} %sweep.6._.refs_0_), channel_id=1, source_target_pairs={{0,2},{2,64},{64,66},{66,128},{128,130},{130,192},{192,194},{194,2... | collective-permute-start | bytes 2359304 | tf_op jit(solution)/shard_map/ppermute | solution.py:389
  143.7 13.1 %collective-permute-start.11 = (f32[1536,128]{1,0:T(8,128)S(1)}, f32[1536,128]{1,0:T(8,128)S(1)}, u32[]{:S(2)}, u32[]{:S(2)}) collective-permute-start(f32[1536,128]{1,0:T(8,128)S(1)} %sweep.6._.refs_0_), channel_id=1, source_target_pairs={{2,0},{64,2},{66,64},{128,66},{130,128},{192,130},{194,192},{208,1... | collective-permute-start | bytes 2359304 | tf_op jit(solution)/shard_map/ppermute | solution.py:389
  149.0 10.7 %collective-permute-start.14 = (f32[1024,128]{1,0:T(8,128)S(1)}, f32[1024,128]{1,0:T(8,128)S(1)}, u32[]{:S(2)}, u32[]{:S(2)}) collective-permute-start(f32[1024,128]{1,0:T(8,128)S(1)} %sweep.7._.refs_0_), channel_id=1, source_target_pairs={{0,2},{2,64},{64,66},{66,128},{128,130},{130,192},{192,194},{194,2... | collective-permute-start | bytes 1572872 | tf_op jit(solution)/shard_map/ppermute | solution.py:389
  149.1 13.4 %collective-permute-start.13 = (f32[1024,128]{1,0:T(8,128)S(1)}, f32[1024,128]{1,0:T(8,128)S(1)}, u32[]{:S(2)}, u32[]{:S(2)}) collective-permute-start(f32[1024,128]{1,0:T(8,128)S(1)} %sweep.7._.refs_0_), channel_id=1, source_target_pairs={{2,0},{64,2},{66,64},{128,66},{130,128},{192,130},{194,192},{208,1... | collective-permute-start | bytes 1572872 | tf_op jit(solution)/shard_map/ppermute | solution.py:389
  157.7 10.4 %collective-permute-start.16 = (f32[1536,128]{1,0:T(8,128)S(1)}, f32[1536,128]{1,0:T(8,128)S(1)}, u32[]{:S(2)}, u32[]{:S(2)}) collective-permute-start(f32[1536,128]{1,0:T(8,128)S(1)} %sweep.8._.refs_0_), channel_id=1, source_target_pairs={{0,2},{2,64},{64,66},{66,128},{128,130},{130,192},{192,194},{194,2... | collective-permute-start | bytes 2359304 | tf_op jit(solution)/shard_map/ppermute | solution.py:389
  157.8 13.1 %collective-permute-start.15 = (f32[1536,128]{1,0:T(8,128)S(1)}, f32[1536,128]{1,0:T(8,128)S(1)}, u32[]{:S(2)}, u32[]{:S(2)}) collective-permute-start(f32[1536,128]{1,0:T(8,128)S(1)} %sweep.8._.refs_0_), channel_id=1, source_target_pairs={{2,0},{64,2},{66,64},{128,66},{130,128},{192,130},{194,192},{208,1... | collective-permute-start | bytes 2359304 | tf_op jit(solution)/shard_map/ppermute | solution.py:389
  163.0 10.7 %collective-permute-start.18 = (f32[1024,128]{1,0:T(8,128)S(1)}, f32[1024,128]{1,0:T(8,128)S(1)}, u32[]{:S(2)}, u32[]{:S(2)}) collective-permute-start(f32[1024,128]{1,0:T(8,128)S(1)} %sweep.9._.refs_0_), channel_id=1, source_target_pairs={{0,2},{2,64},{64,66},{66,128},{128,130},{130,192},{192,194},{194,2... | collective-permute-start | bytes 1572872 | tf_op jit(solution)/shard_map/ppermute | solution.py:389
  163.1 13.4 %collective-permute-start.17 = (f32[1024,128]{1,0:T(8,128)S(1)}, f32[1024,128]{1,0:T(8,128)S(1)}, u32[]{:S(2)}, u32[]{:S(2)}) collective-permute-start(f32[1024,128]{1,0:T(8,128)S(1)} %sweep.9._.refs_0_), channel_id=1, source_target_pairs={{2,0},{64,2},{66,64},{128,66},{130,128},{192,130},{194,192},{208,1... | collective-permute-start | bytes 1572872 | tf_op jit(solution)/shard_map/ppermute | solution.py:389
  172.9 13.8 %collective-permute-start.21 = (f32[1152,128]{1,0:T(8,128)S(1)}, f32[1152,128]{1,0:T(8,128)S(1)}, u32[]{:S(2)}, u32[]{:S(2)}) collective-permute-start(f32[1152,128]{1,0:T(8,128)S(1)} %get-tuple-element.36.refs_0_), channel_id=1, source_target_pairs={{0,2},{2,64},{64,66},{66,128},{128,130},{130,192},{192,194},{194,2... | collective-permute-start | bytes 1769480 | tf_op jit(solution)/shard_map/ppermute | solution.py:389
  173.0 13.8 %collective-permute-start.19 = (f32[1152,128]{1,0:T(8,128)S(1)}, f32[1152,128]{1,0:T(8,128)S(1)}, u32[]{:S(2)}, u32[]{:S(2)}) collective-permute-start(f32[1152,128]{1,0:T(8,128)S(1)} %get-tuple-element.36.refs_0_), channel_id=1, source_target_pairs={{2,0},{64,2},{66,64},{128,66},{130,128},{192,130},{194,192},{208,1... | collective-permute-start | bytes 1769480 | tf_op jit(solution)/shard_map/ppermute | solution.py:389
  177.9 8.8 %collective-permute-start.20 = (f32[768,128]{1,0:T(8,128)S(1)}, f32[768,128]{1,0:T(8,128)S(1)}, u32[]{:S(2)}, u32[]{:S(2)}) collective-permute-start(f32[768,128]{1,0:T(8,128)S(1)} %get-tuple-element.38.refs_1_), channel_id=1, source_target_pairs={{2,0},{64,2},{66,64},{128,66},{130,128},{192,130},{194,192},{208,1... | collective-permute-start | bytes 1179656 | tf_op jit(solution)/shard_map/ppermute | solution.py:389
  (16 other events, 233.3 us)
